TPU v7x, 32 devices: a whole 2x2x4 slice. The times are simulated.
32 devices in a mesh: gx: 4 (over z), gy: 4 (over x, core), sa: 2 (over y).
Axes of the slice: x: 2, y: 2, z: 4, core: 2. Of those that a mesh axis runs over, the one named last changes fastest.
Arguments:
- field_now: float32 [160, 256, 512], P('sa', 'gy', 'gx'), may hold values from -1.5 to 1.5
- field_before: float32 [160, 256, 512], P('sa', 'gy', 'gx'), may hold values from -1.5 to 1.5
- source: float32 [160, 256, 512], P('sa', 'gy', 'gx'), may hold values from -0.06 to 0.06
- log_fields: float32 [9, 256, 512], P(None, ('gy', 'sa'), 'gx'), may hold values from -0.15 to 0.15
- weights: float32 [1500], replicated, may hold values from 0.0002 to 0.002
- mean_perm: float32 [], replicated, may hold values from 0.5 to 2
- node_index: int32 [1500, 8], replicated, may hold values from 0 to 6
- mode_index: int32 [160, 8], replicated, may hold values from 0 to 3, as said below
Outputs:
- fresh: float32 [160, 256, 512], P('sa', 'gy', 'gx')
- update: float32 [160, 256, 512], P('sa', 'gy', 'gx')
Inputs may be any that keep to these rules, and one draw needn't show every extreme that they name: `node_index`: each entry numbers a point of the list in the first step. `mode_index`: the rows are distinct multi-indices of total degree at most 3.
All inputs are finite; a program needn't handle non-finite values.
Results may differ from a plain program's by a relative error of at most 0.0003.
Values sent between devices are 32-bit elements; how exact they have to be, the bound alone decides.
A program may use at most 128 MiB of HBM per device.

v0:
```python
import functools
import math

import jax
import jax.numpy as jnp
import numpy as np
from jax import lax
from jax.experimental import pallas as pl
from jax.experimental.pallas import tpu as pltpu
from jax.sharding import PartitionSpec as P


HIGHEST = lax.Precision.HIGHEST
hermite_points = (
    0.0,
    -1.7320508075688772,
    1.7320508075688772,
    -1.355626179974266,
    1.355626179974266,
    -2.8569700138728056,
    2.8569700138728056,
)
storage_rate = 0.0004
relax_weight = 1.6
step_length = 0.3


LANES = 128
NODE_BLOCK = 512
LOG_DEPTH = 16
BF16 = jnp.bfloat16


def round_up(value, step):
    return -(-value // step) * step


def product(left, right):
    return jnp.dot(left, right, preferred_element_type=jnp.float32)


def split_two(block):
    high = block.astype(BF16)
    return (high, (block - high.astype(jnp.float32)).astype(BF16))


def stacked(parts, depth):
    missing = depth - sum(part.shape[0] for part in parts)
    if missing:
        parts = parts + [jnp.zeros((missing,) + parts[0].shape[1:], parts[0].dtype)]
    return jnp.concatenate(parts, axis=0)


def node_kernel(
    sizes, field_ref, log_ref, field_cols_ref, log_cols_ref, germ_ref, degree_ref, weight_ref,
    out_ref,
    lines, log_lines, log_sides, sides, total, line_op, log_op, basis_op, germ_op, weight_op,
    edge, value_prev, half_prev, flux_prev,
    line_send, line_recv, halo_send, side_send, side_recv, log_send, log_recv, out_send, out_recv,
):
    count_x, count_y, shares, group = sizes
    modes, rows, width = field_ref.shape
    own_rows = rows // shares
    every = shares * modes
    below, above = own_rows, own_rows + 1
    blocks = basis_op.shape[0] // NODE_BLOCK
    x, y, share = (lax.axis_index(axis) for axis in ("gx", "gy", "sa"))
    first_y = jnp.logical_and(y == 0, share == 0)
    last_y = jnp.logical_and(y == count_y - 1, share == shares - 1)
    not_first, not_last = jnp.logical_not(first_y), jnp.logical_not(last_y)
    peer = lambda step: lax.rem(share + step, shares)

    def remote(source, target, send, recv, **place):
        return pltpu.make_async_remote_copy(
            src_ref=source, dst_ref=target, send_sem=send, recv_sem=recv,
            device_id=place, device_id_type=pl.DeviceIdType.MESH,
        )

    def arrived(target, recv):
        pltpu.make_async_copy(target, target, recv).wait()

    barrier = pltpu.get_barrier_semaphore()
    greet = lambda **place: pl.semaphore_signal(
        barrier, inc=1, device_id=place, device_id_type=pl.DeviceIdType.MESH
    )
    for step in range(1, shares):
        greet(sa=peer(step))
    conditions = (
        (x > 0, dict(gx=x - 1)), (x < count_x - 1, dict(gx=x + 1)),
        (y > 0, dict(gy=y - 1)), (y < count_y - 1, dict(gy=y + 1)),
    )
    for condition, place in conditions:
        @pl.when(condition)
        def _():
            for step in range(shares):
                greet(sa=peer(step), **place)
    sides_met = sum(condition.astype(jnp.int32) for condition, _ in conditions)
    pl.semaphore_wait(barrier, shares - 1 + shares * sides_met)

    remote_copies = []

    def start(condition, copy):
        remote_copies.append((condition, copy))
        if condition is None:
            copy.start()
        else:
            pl.when(condition)(copy.start)

    row_of = lambda row: field_ref.at[:, row, :]
    flat_next = jnp.where(share == shares - 1, y + 1, y), lax.rem(share + 1, shares)
    flat_last = jnp.where(share == 0, y - 1, y), lax.rem(share + shares - 1, shares)
    log_copies = (
        (not_last, log_ref.at[:, own_rows - 1, :], log_lines.at[1], 0,
         dict(gy=flat_next[0], sa=flat_next[1])),
        (not_first, log_ref.at[:, 0, :], log_lines.at[0], 1,
         dict(gy=flat_last[0], sa=flat_last[1])),
        (x < count_x - 1, log_cols_ref.at[1], log_sides.at[0], 2, dict(gx=x + 1)),
        (x > 0, log_cols_ref.at[0], log_sides.at[1], 3, dict(gx=x - 1)),
    )
    for condition, source, target, slot, place in log_copies:
        start(condition, remote(source, target, log_send.at[slot], log_recv.at[slot], **place))
    start(y > 0, remote(
        row_of(0), lines.at[below, share], halo_send.at[0], line_recv.at[below, share],
        gy=y - 1, sa=jnp.int32(shares - 1),
    ))
    start(y < count_y - 1, remote(
        row_of(rows - 1), lines.at[above, share], halo_send.at[1], line_recv.at[above, share],
        gy=y + 1, sa=jnp.int32(0),
    ))
    for step in range(1, shares):
        to = peer(step)
        start(to > 0, remote(
            row_of(jnp.maximum(to * own_rows - 1, 0)), lines.at[above, share],
            halo_send.at[2 * step], line_recv.at[above, share], sa=to,
        ))
        start(to < shares - 1, remote(
            row_of(jnp.minimum((to + 1) * own_rows, rows - 1)), lines.at[below, share],
            halo_send.at[2 * step + 1], line_recv.at[below, share], sa=to,
        ))
    own_above = pltpu.make_async_copy(
        row_of(jnp.maximum(share * own_rows - 1, 0)), lines.at[above, share],
        line_recv.at[above, share],
    )
    own_below = pltpu.make_async_copy(
        row_of(jnp.minimum((share + 1) * own_rows, rows - 1)), lines.at[below, share],
        line_recv.at[below, share],
    )
    pl.when(share > 0)(own_above.start)
    pl.when(share < shares - 1)(own_below.start)
    for step in range(shares):
        to = peer(step)
        for kind in range(2):
            source = field_cols_ref.at[to, kind]
            if step:
                start(None, remote(
                    source, sides.at[kind, share], side_send.at[step, kind],
                    side_recv.at[kind, share], sa=to,
                ))
            else:
                pltpu.make_async_copy(
                    source, sides.at[kind, share], side_recv.at[kind, share]
                ).start()
        start(x > 0, remote(
            field_cols_ref.at[to, 0], sides.at[2, share], side_send.at[step, 2],
            side_recv.at[2, share], gx=x - 1, sa=to,
        ))
        start(x < count_x - 1, remote(
            field_cols_ref.at[to, 1], sides.at[3, share], side_send.at[step, 3],
            side_recv.at[3, share], gx=x + 1, sa=to,
        ))

    def line_copy(row, step):
        to = peer(step)
        return remote(
            row_of(to * own_rows + row), lines.at[row, share], line_send.at[row, step],
            line_recv.at[row, share], sa=to,
        )

    def send_lines(row, carry):
        for step in range(1, shares):
            line_copy(row, step).start()
        pltpu.make_async_copy(
            row_of(share * own_rows + row), lines.at[row, share], line_recv.at[row, share]
        ).start()
        return carry

    lax.fori_loop(0, own_rows, send_lines, 0)

    weight_op[...] = jnp.zeros_like(weight_op)
    total[...] = jnp.zeros_like(total)

    def make_basis(block, carry):
        lanes = pl.ds(pl.multiple_of(block * LANES, LANES), LANES)
        germs = germ_ref[:, lanes]
        square = germs * germs
        second = (square - 1.0) / math.sqrt(2.0)
        third = (square * germs - 3.0 * germs) / math.sqrt(6.0)
        values = jnp.ones((every, LANES), jnp.float32)
        for germ in range(germs.shape[0]):
            degree = jnp.broadcast_to(degree_ref[:, germ : germ + 1], (every, LANES))
            at = lambda table: jnp.broadcast_to(table[germ : germ + 1, :], (every, LANES))
            values = values * jnp.where(
                degree == 0, 1.0,
                jnp.where(degree == 1, at(germs), jnp.where(degree == 2, at(second), at(third))),
            )
        high, low = split_two(values)
        wide = lambda a: a.astype(jnp.float32)
        stack = stacked([wide(high), wide(high), wide(low)], basis_op.shape[1])
        basis_op[lanes, :] = jnp.transpose(stack).astype(BF16)
        high, low = split_two(values * (2.0 * weight_ref[:, lanes]))
        weight_op[:every, lanes] = high
        weight_op[every:, lanes] = low
        spread = stacked([-jnp.ones((1, LANES), jnp.float32), -germs], LOG_DEPTH)
        high, low = split_two(spread)
        stack = stacked([wide(high), wide(high), wide(low)], LANES)
        germ_op[lanes, :] = jnp.transpose(stack).astype(BF16)
        return carry

    lax.fori_loop(0, basis_op.shape[0] // LANES, make_basis, 0)

    def log_stack(block):
        high, low = split_two(stacked([block], LOG_DEPTH))
        return stacked([high, low, high], LANES)

    def field_stack(block):
        high, low = split_two(block)
        return stacked([high, low, high], line_op.shape[1])

    for condition, _, target, slot, _ in (
        (not_first, None, log_lines.at[1], 0, None), (not_last, None, log_lines.at[0], 1, None),
        (x > 0, None, log_sides.at[0], 2, None), (x < count_x - 1, None, log_sides.at[1], 3, None),
    ):
        @pl.when(condition)
        def _():
            arrived(target, log_recv.at[slot])

    def make_log(row, carry):
        log_op[row] = log_stack(log_ref[:, row, :])
        return carry

    lax.fori_loop(0, own_rows, make_log, 0)
    log_op[below] = log_stack(
        jnp.where(last_y, log_ref[:, own_rows - 1, :], log_lines[0])
    )
    log_op[above] = log_stack(jnp.where(first_y, log_ref[:, 0, :], log_lines[1]))

    def at_nodes(nodes, field, logs):
        return (product(basis_op[nodes, :], field), jnp.exp(product(germ_op[nodes, :], logs)))

    def flux(later, earlier, half_later, half_earlier):
        return (later - earlier) * pl.reciprocal(half_later + half_earlier)

    def project(nodes, applied):
        high = applied.astype(BF16)
        rest = applied - high.astype(jnp.float32)
        middle = rest.astype(BF16)
        low = (rest - middle.astype(jnp.float32)).astype(BF16)
        both = product(weight_op[:, nodes], high) + product(weight_op[:, nodes], middle)
        return both[:every] + both[every:] + product(weight_op[:every, nodes], low)

    node_slice = lambda block: pl.ds(pl.multiple_of(block * NODE_BLOCK, NODE_BLOCK), NODE_BLOCK)

    for kind in range(4):
        condition = (None, None, x < count_x - 1, x > 0)[kind]
        for source in range(shares):
            wait = lambda: arrived(sides.at[kind, source], side_recv.at[kind, source])
            wait() if condition is None else pl.when(condition)(wait)
    flat = lambda ref: ref.reshape(every, LANES)
    side = [flat(sides[kind]) for kind in range(4)]
    log_first, log_last = log_cols_ref[0], log_cols_ref[1]
    before = jnp.where(x == 0, side[0], side[3])
    after = jnp.where(x == count_x - 1, side[1], side[2])
    log_before = jnp.where(x == 0, log_first, log_sides[0])
    log_after = jnp.where(x == count_x - 1, log_last, log_sides[1])

    def beside(low_part, high_part):
        lane = lax.broadcasted_iota(jnp.int32, low_part.shape, 1)
        return jnp.where(lane < own_rows, low_part, pltpu.roll(high_part, own_rows, 1))

    line_op[0, :, :LANES] = field_stack(beside(before, side[1]))
    line_op[0, :, LANES:] = field_stack(beside(side[0], after))
    log_edge = jnp.concatenate(
        [log_stack(beside(log_before, log_last)), log_stack(beside(log_first, log_after))], axis=1
    )
    edge[...] = jnp.zeros_like(edge)

    def make_edge(block, carry):
        nodes = node_slice(block)
        values, halves = at_nodes(nodes, line_op[0], log_edge)
        edge[...] += project(nodes, flux(
            values[:, LANES:], values[:, :LANES], halves[:, LANES:], halves[:, :LANES]
        ))
        return carry

    lax.fori_loop(0, blocks, make_edge, 0)

    def wait_line(row):
        for source in range(shares):
            arrived(lines.at[row, source], line_recv.at[row, source])

    wait_line(0)
    pl.when(not_first)(lambda: wait_line(above))
    line = flat(lines[0])
    line_op[0, :, :LANES] = field_stack(jnp.where(first_y, line, flat(lines[above])))
    line_op[0, :, LANES:] = field_stack(line)

    def begin(block, carry):
        nodes = node_slice(block)
        logs = jnp.concatenate([log_op[above], log_op[0]], axis=1)
        values, halves = at_nodes(nodes, line_op[0], logs)
        value_prev[nodes, :] = values[:, LANES:]
        half_prev[nodes, :] = halves[:, LANES:]
        flux_prev[nodes, :] = flux(
            values[:, LANES:], values[:, :LANES], halves[:, LANES:], halves[:, :LANES]
        )
        return carry

    lax.fori_loop(0, blocks, begin, 0)

    def out_copy(row, step):
        to = peer(step)
        return remote(
            total.at[row, to], out_ref.at[:, share * own_rows + row, :], out_send.at[row, step],
            out_recv.at[row, share], sa=to,
        )

    def own_copy(row):
        return pltpu.make_async_copy(
            total.at[row, share], out_ref.at[:, share * own_rows + row, :],
            out_recv.at[row, share],
        )

    def take_group(index, carry):
        base = index * group
        for ahead in range(1, group + 1):
            row = base + ahead
            if ahead < group:
                wait_line(row)
            else:
                pl.when(jnp.logical_or(row < own_rows, not_last))(lambda: wait_line(row))
            line = flat(lines[row])
            if ahead == group:
                line = jnp.where(
                    jnp.logical_and(row == own_rows, last_y), flat(lines[row - 1]), line
                )
            place = pl.ds((ahead - 1) % 2 * LANES, LANES)
            line_op[(ahead - 1) // 2, :, place] = field_stack(line)

        def take_nodes(block, carry):
            nodes = node_slice(block)
            value, half, flux_up = value_prev[nodes, :], half_prev[nodes, :], flux_prev[nodes, :]
            inside = lax.broadcasted_iota(jnp.int32, value.shape, 1) < LANES - 1
            for pair in range(group // 2):
                row = base + 2 * pair
                logs = jnp.concatenate([log_op[row + 1], log_op[row + 2]], axis=1)
                values, halves = at_nodes(nodes, line_op[pair], logs)
                applied = []
                for here in range(2):
                    value_next = values[:, here * LANES : (here + 1) * LANES]
                    half_next = halves[:, here * LANES : (here + 1) * LANES]
                    flux_down = flux(value_next, value, half_next, half)
                    across = jnp.where(
                        inside,
                        flux(
                            pltpu.roll(value, LANES - 1, 1), value,
                            pltpu.roll(half, LANES - 1, 1), half,
                        ),
                        0.0,
                    )
                    applied.append(
                        (0.5 * storage_rate) * value
                        - (across - pltpu.roll(across, 1, 1)) - (flux_down - flux_up)
                    )
                    value, half, flux_up = value_next, half_next, flux_down
                sums = project(nodes, jnp.concatenate(applied, axis=1))
                parts = sums.reshape(shares, modes, 2 * LANES)
                total[row] += parts[:, :, :LANES]
                total[row + 1] += parts[:, :, LANES:]
            value_prev[nodes, :] = value
            half_prev[nodes, :] = half
            flux_prev[nodes, :] = flux_up
            return carry

        lax.fori_loop(0, blocks, take_nodes, 0)
        lane = lax.broadcasted_iota(jnp.int32, (every, LANES), 1)
        for step in range(group):
            row = base + step
            left = pltpu.roll(edge[...], lax.rem(LANES - row, LANES), 1)
            right = pltpu.roll(edge[...], LANES - 1 - own_rows - row, 1)
            change = jnp.where(lane == 0, left, 0.0) - jnp.where(lane == LANES - 1, right, 0.0)
            total[row] += change.reshape(shares, modes, LANES)
        for step in range(group):
            row = base + step
            for to in range(1, shares):
                out_copy(row, to).start()
            own_copy(row).start()
        return carry

    lax.fori_loop(0, own_rows // group, take_group, 0)

    def finish(row, carry):
        for step in range(1, shares):
            line_copy(row, step).wait_send()
            out_copy(row, step).wait_send()
            source = peer(step)
            arrived(out_ref.at[:, source * own_rows + row, :], out_recv.at[row, source])
        own_copy(row).wait()
        return carry

    lax.fori_loop(0, own_rows, finish, 0)
    for condition, copy in remote_copies:
        if condition is None:
            copy.wait_send()
        else:
            pl.when(condition)(copy.wait_send)


def galerkin_product(field, log_fields, weights, node_index, mode_index):
    modes, rows, width = field.shape
    count_x, count_y, shares = (lax.axis_size(axis) for axis in ("gx", "gy", "sa"))
    padded = round_up(modes, 16)
    grow = lambda a, size, dim: jnp.pad(
        a, [(0, size - a.shape[d] if d == dim else 0) for d in range(a.ndim)]
    )
    field = grow(field, padded, 0)
    own_rows = rows // shares
    nodes = node_index.shape[0]
    all_nodes = round_up(nodes, NODE_BLOCK)
    germs = grow(node_germs(node_index).T, all_nodes, 1)
    degrees = grow(mode_index.reshape(shares, modes, -1), padded, 1).reshape(shares * padded, -1)
    cols = jnp.stack([field[:, :, 0], field[:, :, -1]]).reshape(2, padded, shares, own_rows)
    cols = grow(cols.transpose(2, 0, 1, 3), LANES, 3)
    log_cols = grow(jnp.stack([log_fields[:, :, 0], log_fields[:, :, -1]]), LANES, 2)
    levels = log_fields.shape[0]
    group = math.gcd(own_rows, 8)
    every = shares * padded
    depth = round_up(3 * every, LANES)
    slots = own_rows + 2
    vmem = lambda shape, kind=jnp.float32: pltpu.VMEM(shape, kind)
    dma = lambda *shape: pltpu.SemaphoreType.DMA(shape)
    place = pl.BlockSpec(memory_space=pl.ANY)
    whole = pl.BlockSpec(memory_space=pltpu.VMEM)
    result = pl.pallas_call(
        functools.partial(node_kernel, (count_x, count_y, shares, group)),
        in_specs=[place, whole, place, whole, whole, whole, whole],
        out_specs=place,
        out_shape=jax.ShapeDtypeStruct((padded, rows, width), jnp.float32),
        scratch_shapes=[
            vmem((slots, shares, padded, LANES)),
            vmem((2, levels, LANES)),
            vmem((2, levels, LANES)),
            vmem((4, shares, padded, LANES)),
            vmem((own_rows, shares, padded, LANES)),
            vmem((group // 2, depth, 2 * LANES), BF16),
            vmem((slots, LANES, LANES), BF16),
            vmem((all_nodes, depth), BF16),
            vmem((all_nodes, LANES), BF16),
            vmem((2 * every, all_nodes), BF16),
            vmem((every, LANES)),
            vmem((all_nodes, LANES)),
            vmem((all_nodes, LANES)),
            vmem((all_nodes, LANES)),
            dma(own_rows, shares), dma(slots, shares), dma(2 * shares), dma(shares, 4),
            dma(4, shares), dma(4), dma(4), dma(own_rows, shares), dma(own_rows, shares),
        ],
        compiler_params=pltpu.CompilerParams(
            collective_id=0, has_side_effects=True, vmem_limit_bytes=56 * 1024 * 1024
        ),
    )(
        field, log_fields, cols, log_cols, germs, degrees,
        grow(weights[None, :], all_nodes, 1),
    )
    return result[:modes]


def node_germs(node_index):
    levels = jnp.arange(len(hermite_points), dtype=jnp.int32)
    picked = (node_index[:, :, None] == levels).astype(jnp.float32)
    points = jnp.asarray(hermite_points, dtype=jnp.float32)
    return jnp.sum(picked * points, axis=2)


def on_device(
    field_now, field_before, source, log_fields, weights, mean_perm, node_index, mode_index
):
    galerkin = galerkin_product(field_now, log_fields, weights, node_index, mode_index)
    update = precondition(source - galerkin, mean_perm)
    fresh = field_before + relax_weight * (field_now - field_before + step_length * update)
    return (fresh, update)


def cosine_table(length):
    freq, cells = np.arange(length)[:, None], np.arange(length)[None, :]
    factor = np.where(freq == 0, math.sqrt(1.0 / length), math.sqrt(2.0 / length))
    return factor * np.cos((freq * (2 * cells + 1) % (4 * length)) * (math.pi / (2 * length)))


def flux_table(count, mean_perm, inverse, ends):
    same = jnp.sum(inverse * ends[0] * ends[0], axis=0)
    cross = jnp.sum(inverse * ends[0] * ends[1], axis=0)
    number = np.arange(1, count)
    sines = np.sin((number[:, None] * number[None, :]) % (2 * count) * (math.pi / count))
    pairs = (2.0 / count) * sines[:, :, None] * sines[:, None, :]
    turns = np.cos(number * (math.pi / count))
    shrink = 1.0 / (1.0 / mean_perm + 2.0 * same - 2.0 * cross * turns[:, None].astype(np.float32))
    table = jnp.sum(pairs[:, :, :, None].astype(np.float32) * shrink[:, None, None, :], axis=0)
    return jnp.pad(table, ((1, 1), (0, 0), (0, 0)))


def precondition(residual, mean_perm):
    gy, gx = (lax.axis_size(axis) for axis in ("gy", "gx"))
    modes, rows, width = residual.shape
    f32 = lambda a: jnp.asarray(a.astype(np.float32))
    row_table, col_table, whole_table = (cosine_table(n) for n in (rows, width, gx * width))
    rows_matrix, cols_matrix = f32(row_table), f32(col_table)
    row_ends, col_ends = f32(row_table[:, [0, -1]].T), f32(col_table[:, [0, -1]].T)
    join = f32(np.einsum("kix,lx->kil", whole_table.reshape(-1, gx, width), col_table))
    eigen = lambda count: 2.0 - 2.0 * np.cos(np.arange(count) * (math.pi / count))
    denominator = lambda cols: storage_rate + mean_perm * f32(eigen(rows)[:, None] + cols[None, :])
    inverse = 1.0 / denominator(eigen(width))
    col_flux = flux_table(gx, mean_perm, inverse.T, col_ends[:, :, None])
    row_flux = flux_table(gy, mean_perm, 1.0 / denominator(eigen(gx * width)), row_ends[:, :, None])
    mix = lambda spec, *args: jnp.einsum(spec, *args, precision=HIGHEST)

    spectral = mix("jy,myx->mjx", rows_matrix, residual)
    spectral = mix("mjx,kx->mjk", spectral, cols_matrix)
    alone = spectral * inverse
    at_cols = mix("mjk,ck->mcj", alone, col_ends)
    at_rows = mix("mjk,cj->mck", alone, row_ends)
    sides = jnp.concatenate([at_cols.reshape(modes, -1), at_rows.reshape(modes, -1)], axis=1)
    part = -(-modes // (gx * gy))
    sides = jnp.pad(sides, ((0, gx * gy * part - modes), (0, 0)))
    swap = lambda a: lax.all_to_all(a, ("gx", "gy"), split_axis=0, concat_axis=0, tiled=True)
    every = swap(sides).reshape(gx, gy, part, -1)

    def col_fluxes(ends):
        jump = ends[1:, :, :, 0] - ends[:-1, :, :, 1]
        return jnp.sum(col_flux[:, :, None, None, :] * jump[None], axis=1)

    at_cols = every[..., : 2 * rows].reshape(gx, gy, part, 2, rows)
    at_rows = every[..., 2 * rows :].reshape(gx, gy, part, 2, width)
    through_cols = col_fluxes(at_cols)
    by_row = inverse * row_ends[:, :, None]
    by_col = inverse * col_ends[:, None, :]
    at_rows = (
        at_rows
        + mix("iymj,cjk->iymck", through_cols[1:], by_row) * col_ends[1]
        - mix("iymj,cjk->iymck", through_cols[:-1], by_row) * col_ends[0]
    )
    jump = at_rows[:, 1:, :, 0] - at_rows[:, :-1, :, 1]
    jump = mix("kil,iyml->ymk", join, jump)
    through_rows = jnp.sum(row_flux[:, :, None, :] * jump[None], axis=1)
    through_rows = mix("kil,ymk->iyml", join, through_rows)
    back = mix("iymk,cjk->iymcj", through_rows, by_col)
    through_cols = through_cols + col_fluxes(
        back[:, 1:] * row_ends[1] - back[:, :-1] * row_ends[0]
    )
    through = jnp.concatenate(
        [through_cols[:-1], through_cols[1:], through_rows[:, :-1], through_rows[:, 1:]], axis=-1
    )
    through = swap(through.reshape(gx * gy * part, -1))[:modes, None, :]
    left, right = through[..., :rows], through[..., rows : 2 * rows]
    top, bottom = through[..., 2 * rows : -width], through[..., -width:]
    upright = lambda a: jnp.swapaxes(a, 1, 2)
    spectral = spectral + (upright(right) * col_ends[1] - upright(left) * col_ends[0])
    spectral = spectral + (bottom * row_ends[1][:, None] - top * row_ends[0][:, None])
    spectral = spectral * inverse
    columns = mix("mjk,kx->mjx", spectral, cols_matrix)
    return mix("jy,mjx->myx", rows_matrix, columns)


def solution(mesh):
    return jax.shard_map(
        on_device,
        mesh=mesh,
        in_specs=(
            P("sa", "gy", "gx"),
            P("sa", "gy", "gx"),
            P("sa", "gy", "gx"),
            P(None, ("gy", "sa"), "gx"),
            P(),
            P(),
            P(),
            P(),
        ),
        out_specs=(P("sa", "gy", "gx"), P("sa", "gy", "gx")),
        check_vma=False,
    )
```

profile of v0, /device:TPU:0, one launch (start us, length us, event | category | flops | bytes accessed | tf_op | source)
XLA Modules:
  0.0 145.3 jit_solution(11262188424043293782)
XLA Ops:
  1.3 0.7 broadcast_in_dim.4
  2.0 0.6 pad.27.weight_ref
  2.6 0.9 select_reduce_fusion
  3.5 0.6 pad.26.germ_ref
  4.1 1.4 copy.64.degree_ref
  5.6 1.1 fusion.58
  6.7 0.2 copy.93
  6.8 0.2 copy.94
  7.0 5.1 %fusion.57 = (f32[80,64,1]{2,1,0:T(8,128)}, f32[80,64,1]{2,1,0:T(8,128)S(1)}) fusion(f32[80,64,128]{2,1,0:T(8,128)} %field_ref.1), kind=kLoop, calls=%fused_computation.95 | loop fusion | bytes 81920 | tf_op jit(solution)/shard_map/slice | solution.py:431
  12.1 3.0 %copy.91 = f32[80,64,1]{0,1,2:T(8,128)S(1)} copy(f32[80,64,1]{2,1,0:T(8,128)} %get-tuple-element.6) | data formatting | bytes 40960
  15.1 1.6 %copy.92 = f32[80,64,1]{0,1,2:T(8,128)S(1)} copy(f32[80,64,1]{2,1,0:T(8,128)S(1)} %get-tuple-element.7) | data formatting | bytes 40960
  16.8 0.1 copy.61
  16.9 0.7 pad.24.field_cols_ref
  17.6 0.6 select_maximum_fusion.log_cols_ref
  18.2 72.2 %shard_map.203 = f32[80,64,128]{2,1,0:T(8,128)} custom-call(f32[80,64,128]{2,1,0:T(8,128)} %field_ref.1, f32[9,32,128]{2,1,0:T(8,128)} %log_ref.1, f32[2,2,80,128]{3,2,1,0:T(8,128)} %pad.24.field_cols_ref, f32[2,9,128]{2,1,0:T(8,128)} %select_maximum_fusion.log_cols_ref, f32[8,1536]{1,0:T(8,128)} %pad.26.germ_ref, s32[160,8]{1,0:T(8,128)} %copy.64.degree_ref, ...), custom_call_target="tpu_custom_call" | custom-call | tf_op jit(solution)/shard_map/pallas_call | solution.py:443
  90.5 4.4 %fusion.12 = f32[80,128,64]{1,2,0:T(8,128)S(1)} fusion(f32[64,64,1]{1,0,2:T(8,128)S(1)} %copy-done.4, f32[80,64,128]{2,1,0:T(8,128)S(1)} %copy-done.2, f32[80,64,128]{2,1,0:T(8,128)} %shard_map.203), kind=kOutput, calls=%fused_computation.13 | convolution fusion | flops 503971840 | bytes 7880704 | tf_op jit(solution)/shard_map/jy,myx->mjx/dot_general | solution.py:523
  94.9 0.0 copy-start.7
  94.9 0.0 copy-start.10
  94.9 0.0 copy-start.11
  94.9 0.0 copy-start.16
  95.0 2.2 %fusion = f32[80,64,128]{2,1,0:T(8,128)S(1)} fusion(f32[128,128,1]{1,0,2:T(8,128)S(1)} %copy-done.6, f32[80,128,64]{1,2,0:T(8,128)S(1)} %fusion.12), kind=kOutput, calls=%fused_computation | convolution fusion | flops 1006632960 | bytes 5308416 | tf_op jit(solution)/shard_map/mjx,kx->mjk/dot_general | solution.py:523
  97.2 0.1 multiply_reduce_fusion.7
  97.3 1.6 %fusion.34 = f32[80,2,128]{2,1,0:T(2,128)S(1)} fusion(f32[2,64,1]{1,0,2:T(2,128)S(1)} %copy-done.16, f32[80,64,128]{2,1,0:T(8,128)S(1)} %fusion, f32[64,128]{1,0:T(8,128)S(1)} %get-tuple-element.20), kind=kOutput, calls=%fused_computation.36 | convolution fusion | flops 16384000 | bytes 2736640 | tf_op jit(solution)/shard_map/mjk,cj->mck/dot_general | solution.py:523
  99.0 0.1 concatenate.13
  99.1 6.2 %fusion.31 = f32[80,2,64]{2,1,0:T(2,128)S(1)} fusion(f32[2,128,1]{1,0,2:T(2,128)S(1)} %copy-done.15, f32[80,64,128]{2,1,0:T(8,128)S(1)} %fusion, f32[64,128]{1,0:T(8,128)S(1)} %get-tuple-element.20), kind=kOutput, calls=%fused_computation.35 | convolution fusion | flops 16384000 | bytes 2696192 | tf_op jit(solution)/shard_map/mjk,ck->mcj/dot_general | solution.py:523
  105.2 0.1 concatenate.12
  105.4 0.7 pad_maximum_fusion
  106.1 5.1 %all-to-all-start = ((f32[16,5,384]{2,1,0:T(8,128)}), f32[16,5,384]{2,1,0:T(8,128)S(1)}, u32[]{:S(2)}, u32[]{:S(2)}) async-start(f32[16,5,384]{2,1,0:T(8,128)} %pad_maximum_fusion), calls=%async_computation | async-start | bytes 393216 | tf_op jit(solution)/shard_map/all_to_all | solution.py:533
  111.3 0.1 multiply_reduce_fusion.4
  111.4 0.1 subtract_divide_fusion
  111.5 0.1 multiply_reduce_fusion.5
  111.6 0.1 subtract_divide_fusion.1
  111.7 0.1 multiply_reduce_fusion.8
  111.8 8.4 %all-to-all-done = f32[16,5,384]{2,1,0:T(8,128)S(1)} async-done(((f32[16,5,384]{2,1,0:T(8,128)}), f32[16,5,384]{2,1,0:T(8,128)S(1)}, u32[]{:S(2)}, u32[]{:S(2)}) %all-to-all-start) | async-done | bytes 122912 | tf_op jit(solution)/shard_map/all_to_all | solution.py:533
  120.2 0.1 reshape.174
  120.4 0.1 multiply_reduce_fusion.2
  120.5 0.3 convolution_multiply_fusion
  120.8 0.3 fusion.30
  121.2 2.2 %convolution_bitcast_fusion.1 = f32[3,5,512]{2,0,1:T(4,128)S(1)} fusion(f32[512,4,128,1]{2,0,1,3:T(8,128)} %constant.77, f32[4,3,5,128]{3,2,1,0:T(8,128)S(1)} %fusion.49), kind=kOutput, calls=%fused_computation.37 | convolution fusion | flops 47185920 | bytes 1110016 | tf_op jit(solution)/shard_map/kil,iyml->ymk/dot_general | solution.py:523
  123.4 0.1 multiply_reduce_fusion
  123.5 0.7 fusion.40
  124.3 0.3 fusion.38
  124.7 0.1 multiply_reduce_fusion.1
  124.8 0.1 pad_maximum_fusion.1
  125.0 11.6 %all_to_all.15 = f32[16,5,384]{2,1,0:T(8,128)S(1)} all-to-all(f32[16,5,384]{2,1,0:T(8,128)S(1)} %bitcast.89), channel_id=1, replica_groups=mesh['gx'=4,'gy'=4,'sa'=2] {'gx','gy'}, dimensions={0} | all-to-all | bytes 245760 | tf_op jit(solution)/shard_map/all_to_all | solution.py:533
  136.6 0.1 slice_bitcast_fusion.4
  136.6 3.1 %fusion.2 = f32[80,64,128]{2,1,0:T(8,128)S(1)} fusion(f32[128,128,1]{1,0,2:T(8,128)S(1)} %copy-done.6, f32[80,64,128]{2,1,0:T(8,128)S(1)} %fusion, f32[64]{0:T(128)S(1)} %copy-done.13, f32[80,128]{1,0:T(8,128)S(1)} %get-tuple-element.13, f32[64]{0:T(128)S(1)} %copy-done.12, f32[80,128]{1,0:T(8,128)S(1)} %get-tuple-element.12, f32[128]{0:T(128)S(1)} %copy-done.11, ...), kind=kOutput, calls=%fused_computation.3 | convolution fusion | flops 1012531200 | bytes 5465600 | tf_op jit(solution)/shard_map/mjk,kx->mjx/dot_general | solution.py:523
  139.8 5.5 %multiply_add_fusion = (f32[80,64,128]{2,1,0:T(8,128)}, f32[80,64,128]{2,1,0:T(8,128)}) fusion(f32[80,64,128]{2,1,0:T(8,128)S(1)} %copy-done.3, f32[80,64,128]{2,1,0:T(8,128)S(1)} %copy-done, f32[80,64,128]{2,1,0:T(8,128)S(1)} %fusion.2, f32[64,64,1]{1,0,2:T(8,128)S(1)} %copy-done.4), kind=kOutput, calls=%fused_computation.2 | convolution fusion | flops 506593280 | bytes 13123584 | tf_op jit(solution)/shard_map/jy,mjx->myx/dot_general | solution.py:523
  (51 shorter events, 0.3 us)
Async XLA Ops:
  18.2 72.3 %copy-start.2 = (f32[80,64,128]{2,1,0:T(8,128)S(1)}, f32[80,64,128]{2,1,0:T(8,128)}, u32[]{:S(2)}) copy-start(f32[80,64,128]{2,1,0:T(8,128)} %param.22) | copy-start | bytes 7864324
  18.2 72.3 %copy-start.4 = (f32[64,64,1]{1,0,2:T(8,128)S(1)}, f32[64,64,1]{1,0,2:T(8,128)}, u32[]{:S(2)}) copy-start(f32[64,64,1]{1,0,2:T(8,128)} %constant.73) | copy-start | bytes 49156
  90.4 4.5 %copy-start.6 = (f32[128,128,1]{1,0,2:T(8,128)S(1)}, f32[128,128,1]{1,0,2:T(8,128)}, u32[]{:S(2)}) copy-start(f32[128,128,1]{1,0,2:T(8,128)} %constant.74) | copy-start | bytes 196612
  94.9 2.3 %copy-start.7 = (f32[64,128]{1,0:T(8,128)S(1)}, f32[64,128]{1,0:T(8,128)}, u32[]{:S(2)}) copy-start(f32[64,128]{1,0:T(8,128)} %constant.47.clone) | copy-start | bytes 98308
  94.9 2.3 %copy-start.10 = (f32[128]{0:T(128)S(1)}, f32[128]{0:T(128)}, u32[]{:S(2)}) copy-start(f32[128]{0:T(128)} %constant.67) | copy-start | bytes 1540
  94.9 2.3 %copy-start.11 = (f32[128]{0:T(128)S(1)}, f32[128]{0:T(128)}, u32[]{:S(2)}) copy-start(f32[128]{0:T(128)} %constant.65) | copy-start | bytes 1540
  94.9 2.4 %copy-start.16 = (f32[2,64,1]{1,0,2:T(2,128)S(1)}, f32[2,64,1]{1,0,2:T(2,128)}, u32[]{:S(2)}) copy-start(f32[2,64,1]{1,0,2:T(2,128)} %constant.76) | copy-start | bytes 1540
  97.2 1.9 %copy-start.15 = (f32[2,128,1]{1,0,2:T(2,128)S(1)}, f32[2,128,1]{1,0,2:T(2,128)}, u32[]{:S(2)}) copy-start(f32[2,128,1]{1,0,2:T(2,128)} %constant.75) | copy-start | bytes 3076
  98.9 12.3 %copy-start.5 = (f32[64,512]{1,0:T(8,128)S(1)}, f32[64,512]{1,0:T(8,128)}, u32[]{:S(2)}) copy-start(f32[64,512]{1,0:T(8,128)} %constant.50.clone) | copy-start | bytes 393220
  98.9 12.3 %copy-start.12 = (f32[64]{0:T(128)S(1)}, f32[64]{0:T(128)}, u32[]{:S(2)}) copy-start(f32[64]{0:T(128)} %constant.72) | copy-start | bytes 772
  98.9 12.3 %copy-start.13 = (f32[64]{0:T(128)S(1)}, f32[64]{0:T(128)}, u32[]{:S(2)}) copy-start(f32[64]{0:T(128)} %constant.70) | copy-start | bytes 772
  99.0 12.5 %copy-start.14 = (f32[3]{0:T(128)S(1)}, f32[3]{0:T(128)}, u32[]{:S(2)}) copy-start(f32[3]{0:T(128)} %constant.68) | copy-start | bytes 40
  99.0 12.5 %copy-start.8 = (f32[3,3,3]{2,1,0:T(4,128)S(1)}, f32[3,3,3]{2,1,0:T(4,128)}, u32[]{:S(2)}) copy-start(f32[3,3,3]{2,1,0:T(4,128)} %constant.63) | copy-start | bytes 328
  99.0 21.5 %copy-start.9 = (f32[2,64]{1,0:T(2,128)S(1)}, f32[2,64]{1,0:T(2,128)}, u32[]{:S(2)}) copy-start(f32[2,64]{1,0:T(2,128)} %constant.14.clone) | copy-start | bytes 1540
  106.1 18.2 %copy-start.17 = (f32[2,128]{1,0:T(2,128)S(1)}, f32[2,128]{1,0:T(2,128)}, u32[]{:S(2)}) copy-start(f32[2,128]{1,0:T(2,128)} %constant.15.clone) | copy-start | bytes 3076
  106.1 14.1 %all-to-all-start = ((f32[16,5,384]{2,1,0:T(8,128)}), f32[16,5,384]{2,1,0:T(8,128)S(1)}, u32[]{:S(2)}, u32[]{:S(2)}) async-start(f32[16,5,384]{2,1,0:T(8,128)} %pad_maximum_fusion), calls=%async_computation | async-start | bytes 393216 | tf_op jit(solution)/shard_map/all_to_all | solution.py:533
  120.3 3.2 %copy-start.1 = (f32[512,4,128,1]{2,0,1,3:T(8,128)S(1)}, f32[512,4,128,1]{2,0,1,3:T(8,128)}, u32[]{:S(2)}) copy-start(f32[512,4,128,1]{2,0,1,3:T(8,128)} %constant.77) | copy-start | bytes 3145732
  136.6 3.1 %copy-start = (f32[80,64,128]{2,1,0:T(8,128)S(1)}, f32[80,64,128]{2,1,0:T(8,128)}, u32[]{:S(2)}) copy-start(f32[80,64,128]{2,1,0:T(8,128)} %field_ref.1) | copy-start | bytes 7864324
  136.6 3.1 %copy-start.3 = (f32[80,64,128]{2,1,0:T(8,128)S(1)}, f32[80,64,128]{2,1,0:T(8,128)}, u32[]{:S(2)}) copy-start(f32[80,64,128]{2,1,0:T(8,128)} %param.21) | copy-start | bytes 7864324
where the time goes:
time: 146 us; the launch traced here: 145 us
  Pallas kernels  72.2 us (49%)
  matrix products  27 us (18%)
  local copies, waits for them, and re-layouts  15.9 us (11%)
  blocking collectives  11.6 us (8%)
  waiting for transfers between devices  8.37 us (6%)
  starting transfers between devices  5.13 us (4%)
  other arithmetic  3.22 us (2%)
  between operations  1.84 us (1%)
    pallas_call x1, Pallas kernels, galerkin_product(): pl.pallas_call(functools.partial(node_kernel, (count_x, count_y, shares,...  72.2 us
    dot_general x11, matrix products, precondition(): mix = lambda spec, *args: jnp.einsum(spec, *args, precision=HIGHEST)  27 us
    all_to_all x1, blocking collectives, precondition(): lax.all_to_all(a, ('gx', 'gy'), split_axis=0, concat_axis=0, tiled=True)  11.6 us
    all_to_all x1, waiting for transfers between devices, precondition(): lax.all_to_all(a, ('gx', 'gy'), split_axis=0, concat_axis=0, tiled=True)  8.37 us
    unnamed x42, local copies, waits for them, and re-layouts  6.53 us
    all_to_all x1, starting transfers between devices, precondition(): lax.all_to_all(a, ('gx', 'gy'), split_axis=0, concat_axis=0, tiled=True)  5.13 us
    slice x1, local copies, waits for them, and re-layouts, galerkin_product(): field[:, :, 0]  5.12 us
  transfers between devices with their start and end apart: 1, of which 1 were waited for; matrix products, arithmetic and copies ran while one was open for 0% of the time, Pallas kernels for 0%

commit v1 on v0

--- a/solution.py
+++ b/solution.py
@@ -44,6 +44,159 @@
     return (high, (block - high.astype(jnp.float32)).astype(BF16))
 
 
+def split_three(block):
+    high = block.astype(BF16)
+    rest = block - high.astype(jnp.float32)
+    middle = rest.astype(BF16)
+    return (high, middle, (rest - middle.astype(jnp.float32)).astype(BF16))
+
+
+def exact(left, right):
+    return jnp.dot(left, right, precision=HIGHEST, preferred_element_type=jnp.float32)
+
+
+def row_transform(block, pair_ref, rest_ref):
+    high, middle, low = split_three(block)
+    both = product(jnp.concatenate([high, middle], axis=1), pair_ref[...])
+    both = both[:, :LANES] + both[:, LANES:]
+    return both + product(jnp.concatenate([low, high], axis=1), rest_ref[...])
+
+
+def col_transform(block, all_ref):
+    high, middle, low = split_three(block)
+    stack = jnp.concatenate([high, middle, high, middle, low, high], axis=0)
+    return product(all_ref[...], stack)
+
+
+def make_tables(sizes, per, mean, lane_ref, column_ref, far_ref, inverse, by_row, by_col, col_table, row_table):
+    count_x, count_y = sizes
+    half = LANES // 2
+    column = lambda k, rows=LANES: jnp.broadcast_to(column_ref[:rows, k : k + 1], (rows, LANES))
+    lanes = lambda k: lane_ref[k : k + 1, :]
+    upright = 1.0 / (storage_rate + mean * (column(0) + lanes(5)))
+    flat = 1.0 / (storage_rate + mean * (column(3) + lanes(2)))
+    inverse[:, :LANES] = flat[:half]
+    inverse[:, LANES:] = flat[:half]
+    lane = lax.broadcasted_iota(jnp.int32, (LANES, LANES), 1)
+    row = lax.broadcasted_iota(jnp.int32, (LANES, LANES), 0)
+    for end in range(2):
+        part = upright * column(1 + end)
+        by_col[:LANES, end * LANES : (end + 1) * LANES] = jnp.where(lane < half, part, 0.0)
+        by_col[LANES:, end * LANES : (end + 1) * LANES] = jnp.where(lane < half, 0.0, part)
+        part = flat * column(4 + end)
+        by_row[:, 2 * end * LANES : (2 * end + 1) * LANES] = jnp.where(row < half, part, 0.0)
+        by_row[:, (2 * end + 1) * LANES : (2 * end + 2) * LANES] = jnp.where(row < half, 0.0, part)
+
+    def tables(count, same, cross):
+        shrink = [
+            1.0 / (1.0 / mean + 2.0 * same - 2.0 * math.cos(n * math.pi / count) * cross)
+            for n in range(1, count)
+        ]
+        sine = lambda a, b: math.sin(a * b % (2 * count) * math.pi / count)
+        return [
+            [
+                sum((2.0 / count) * sine(n, a) * sine(n, b) * shrink[n - 1] for n in range(1, count))
+                for b in range(1, count)
+            ]
+            for a in range(1, count)
+        ]
+
+    total = lambda a: jnp.sum(a, axis=0, keepdims=True)
+    ends = column(1), column(2)
+    found = tables(
+        count_x, total(upright * ends[0] * ends[0]), total(upright * ends[0] * ends[1])
+    )
+    for a in range(count_x - 1):
+        for b in range(count_x - 1):
+            col_table[a, b : b + 1, :] = found[a][b]
+    far = far_ref[0:1, :]
+    wide = lambda k: jnp.broadcast_to(column_ref[:half, k : k + 1], (half, far.shape[1]))
+    deep = 1.0 / (storage_rate + mean * (wide(3) + far))
+    found = tables(
+        count_y, total(deep * wide(4) * wide(4)), total(deep * wide(4) * wide(5))
+    )
+    depth = row_table.shape[1]
+    where_row = lax.broadcasted_iota(jnp.int32, (depth, far.shape[1]), 0) // per
+    for shift in range(-(count_y - 2), count_y - 1):
+        table = jnp.zeros((depth, far.shape[1]), jnp.float32)
+        for a in range(count_y - 1):
+            if 0 <= a + shift < count_y - 1:
+                table = jnp.where(where_row == a, found[a][a + shift], table)
+        row_table[shift + count_y - 2] = table
+
+
+def solve_fluxes(sizes, per, got, back, lane_ref, join_ref, by_row, by_col, col_table, row_table):
+    count_x, count_y = sizes
+    depth = row_table.shape[1]
+    rows = count_y * per
+    lanes = lambda k: lane_ref[k : k + 1, :]
+    take = lambda block, kind: got[pl.ds(block * rows * 8 + kind, depth, stride=8), :]
+    row = lax.broadcasted_iota(jnp.int32, (depth, LANES), 0)
+    up = lambda a, by=1: pltpu.roll(a, (-by * per) % depth, 0)
+    down = lambda a: jnp.where(row < per, 0.0, pltpu.roll(a, per, 0))
+    blocks, cuts = range(count_x), range(1, count_x)
+
+    def through_cols(first, last):
+        jump = [first[cut] - last[cut - 1] for cut in cuts]
+        return [
+            sum(col_table[a, b : b + 1, :] * jump[b] for b in range(count_x - 1))
+            for a in range(count_x - 1)
+        ]
+
+    fluxes = through_cols([take(b, 0) for b in blocks], [take(b, 1) for b in blocks])
+    spread = [exact(flux, by_row[...]) for flux in fluxes]
+
+    def at_row(block, end, half):
+        part = slice((2 * end + half) * LANES, (2 * end + half + 1) * LANES)
+        value = take(block, 2 + 2 * end + half)
+        if block < count_x - 1:
+            value = value + spread[block][:, part] * lanes(1)
+        if block > 0:
+            value = value - spread[block - 1][:, part] * lanes(0)
+        return value
+
+    jump = jnp.concatenate(
+        [
+            jnp.concatenate([up(at_row(b, 0, half)) - at_row(b, 1, half) for b in blocks], axis=1)
+            for half in range(2)
+        ],
+        axis=0,
+    )
+    far = lax.dot_general(
+        jump, join_ref[...], (((1,), (1,)), ((), ())), precision=HIGHEST,
+        preferred_element_type=jnp.float32,
+    )
+    mixed = []
+    for half in range(2):
+        part = far[half * depth : (half + 1) * depth]
+        mixed.append(sum(
+            row_table[shift + count_y - 2] * (up(part, shift) if shift else part)
+            for shift in range(-(count_y - 2), count_y - 1)
+        ))
+    near = exact(jnp.concatenate(mixed, axis=0), join_ref[...])
+    through_rows = [
+        [near[half * depth : (half + 1) * depth, b * LANES : (b + 1) * LANES] for half in range(2)]
+        for b in blocks
+    ]
+    ends = []
+    for b in blocks:
+        reach = exact(jnp.concatenate(through_rows[b], axis=1), by_col[...])
+        ends.append([
+            lanes(4) * reach[:, end * LANES : (end + 1) * LANES]
+            - lanes(3) * down(reach[:, end * LANES : (end + 1) * LANES])
+            for end in range(2)
+        ])
+    more = through_cols([end[0] for end in ends], [end[1] for end in ends])
+    fluxes = [a + b for a, b in zip(fluxes, more)]
+    nothing = jnp.zeros((depth, LANES), jnp.float32)
+    for b in blocks:
+        left = fluxes[b - 1] if b > 0 else nothing
+        right = fluxes[b] if b < count_x - 1 else nothing
+        top = [down(part) for part in through_rows[b]]
+        for kind, value in enumerate([left, right] + top + through_rows[b]):
+            back[pl.ds(b * rows * 8 + kind, depth, stride=8), :] = value
+
+
 def stacked(parts, depth):
     missing = depth - sum(part.shape[0] for part in parts)
     if missing:
@@ -53,9 +206,13 @@
 
 def node_kernel(
     sizes, field_ref, log_ref, field_cols_ref, log_cols_ref, germ_ref, degree_ref, weight_ref,
-    out_ref,
+    source_ref, mean_ref, pair_ref, rest_ref, all_ref, lane_ref, column_ref, far_ref, join_ref,
+    spec_ref, flux_ref,
     lines, log_lines, log_sides, sides, total, line_op, log_op, basis_op, germ_op, weight_op,
     edge, value_prev, half_prev, flux_prev,
+    home, spectrum, origin, traces, got, back, tall, join,
+    inverse, by_row, by_col, col_table, row_table,
+    load_sem, spec_sem, trace_send, trace_recv, flux_send, flux_recv,
     line_send, line_recv, halo_send, side_send, side_recv, log_send, log_recv, out_send, out_recv,
 ):
     count_x, count_y, shares, group = sizes
@@ -85,6 +242,12 @@
     )
     for step in range(1, shares):
         greet(sa=peer(step))
+    owners = count_x * count_y
+    me = x * count_y + y
+    other = lambda step: lax.rem(me + step, owners)
+    at_owner = lambda owner: dict(gx=lax.div(owner, count_y), gy=lax.rem(owner, count_y))
+    for step in range(1, owners):
+        greet(**at_owner(other(step)))
     conditions = (
         (x > 0, dict(gx=x - 1)), (x < count_x - 1, dict(gx=x + 1)),
         (y > 0, dict(gy=y - 1)), (y < count_y - 1, dict(gy=y + 1)),
@@ -92,10 +255,10 @@
     for condition, place in conditions:
         @pl.when(condition)
         def _():
-            for step in range(shares):
+            for step in range(1, shares):
                 greet(sa=peer(step), **place)
     sides_met = sum(condition.astype(jnp.int32) for condition, _ in conditions)
-    pl.semaphore_wait(barrier, shares - 1 + shares * sides_met)
+    pl.semaphore_wait(barrier, owners - 1 + (shares - 1) * (1 + sides_met))
 
     remote_copies = []
 
@@ -185,6 +348,21 @@
         return carry
 
     lax.fori_loop(0, own_rows, send_lines, 0)
+    load_origin = pltpu.make_async_copy(source_ref, origin, load_sem.at[0])
+    load_origin.start()
+    load_join = pltpu.make_async_copy(join_ref, join, load_sem.at[1])
+    load_join.start()
+    pairs = modes // 2
+    per = traces.shape[0] // 8 // owners
+    plane = (count_x, count_y)
+    beyond = got.shape[0] - traces.shape[0]
+    if beyond:
+        got[traces.shape[0] :, :] = jnp.zeros((beyond, LANES), jnp.float32)
+    traces[...] = jnp.zeros_like(traces)
+    make_tables(
+        plane, per, mean_ref[0], lane_ref, column_ref, far_ref,
+        inverse, by_row, by_col, col_table, row_table,
+    )
 
     weight_op[...] = jnp.zeros_like(weight_op)
     total[...] = jnp.zeros_like(total)
@@ -317,21 +495,36 @@
 
     lax.fori_loop(0, blocks, begin, 0)
 
+    home_row = lambda row: home.at[pl.ds(row * modes, modes), :]
+
     def out_copy(row, step):
         to = peer(step)
         return remote(
-            total.at[row, to], out_ref.at[:, share * own_rows + row, :], out_send.at[row, step],
+            total.at[row, to], home_row(share * own_rows + row), out_send.at[row, step],
             out_recv.at[row, share], sa=to,
         )
 
     def own_copy(row):
         return pltpu.make_async_copy(
-            total.at[row, share], out_ref.at[:, share * own_rows + row, :],
-            out_recv.at[row, share],
-        )
+            total.at[row, share], home_row(share * own_rows + row), out_recv.at[row, share]
+        )
+
+    def take_origin(pair, carry):
+        block = origin[pl.ds(2 * pair, 2)].reshape(2 * rows, LANES)
+        block = row_transform(block, pair_ref, rest_ref)
+        spectrum[pair] = col_transform(
+            jnp.concatenate([block[:rows], block[rows:]], axis=1), all_ref
+        )
+        return carry
+
+    groups = own_rows // group
+    load_origin.wait()
 
     def take_group(index, carry):
         base = index * group
+        lax.fori_loop(
+            lax.div(index * pairs, groups), lax.div((index + 1) * pairs, groups), take_origin, 0
+        )
         for ahead in range(1, group + 1):
             row = base + ahead
             if ahead < group:
@@ -388,7 +581,8 @@
             left = pltpu.roll(edge[...], lax.rem(LANES - row, LANES), 1)
             right = pltpu.roll(edge[...], LANES - 1 - own_rows - row, 1)
             change = jnp.where(lane == 0, left, 0.0) - jnp.where(lane == LANES - 1, right, 0.0)
-            total[row] += change.reshape(shares, modes, LANES)
+            line = row_transform(flat(total[row]) + change, pair_ref, rest_ref)
+            total[row] = line.reshape(shares, modes, LANES)
         for step in range(group):
             row = base + step
             for to in range(1, shares):
@@ -398,31 +592,187 @@
 
     lax.fori_loop(0, own_rows // group, take_group, 0)
 
-    def finish(row, carry):
+    def arrive(row, carry):
+        for step in range(1, shares):
+            source = peer(step)
+            arrived(home_row(source * own_rows + row), out_recv.at[row, source])
+        own_copy(row).wait()
+        return carry
+
+    lax.fori_loop(0, own_rows, arrive, 0)
+
+    def take_pair(pair, columns):
+        line = [home[pl.ds(2 * pair + half, rows, stride=modes), :] for half in range(2)]
+        line = col_transform(jnp.concatenate(line, axis=1), all_ref)
+        line = spectrum[pair] - line
+        spectrum[pair] = line
+        alone = line * inverse[...]
+        trace = pl.ds(8 * pair, 8)
+        lane = lax.broadcasted_iota(jnp.int32, (LANES, LANES), 1)
+        result = []
+        for end in range(2):
+            ends = jnp.broadcast_to(column_ref[:rows, 4 + end : 5 + end], (rows, 2 * LANES))
+            result.append(jnp.sum(alone * ends, axis=0, keepdims=True))
+            upright = jnp.concatenate([alone[:, :LANES], alone[:, LANES:]], axis=0)
+            upright = jnp.sum(upright * lane_ref[end : end + 1, :], axis=1, keepdims=True)
+            columns = jnp.where(lane == end * (LANES // 2) + pair, upright, columns)
+        blank = jnp.zeros((2, LANES), jnp.float32)
+        traces[trace, :] = jnp.concatenate(
+            [blank, result[0][:, :LANES], result[0][:, LANES:],
+             result[1][:, :LANES], result[1][:, LANES:], blank], axis=0
+        )
+        return columns
+
+    columns = lax.fori_loop(0, pairs, take_pair, jnp.zeros((LANES, LANES), jnp.float32))
+    tall[...] = jnp.transpose(columns)
+    for end in range(2):
+        traces[pl.ds(end, pairs, stride=8), :] = tall[pl.ds(end * (LANES // 2), pairs), :]
+    save = pltpu.make_async_copy(spectrum, spec_ref, spec_sem)
+    save.start()
+
+    piece = lambda owner: pl.ds(owner * per * 8, per * 8)
+
+    def trace_copy(step):
+        to = other(step)
+        return remote(
+            traces.at[piece(to), :], got.at[piece(me), :], trace_send.at[step],
+            trace_recv.at[me], **at_owner(to),
+        )
+
+    def flux_copy(step):
+        to = other(step)
+        return remote(
+            back.at[piece(to), :], flux_ref.at[piece(me), :], flux_send.at[step],
+            flux_recv.at[me], **at_owner(to),
+        )
+
+    for step in range(1, owners):
+        trace_copy(step).start()
+    got[piece(me), :] = traces[piece(me), :]
+    load_join.wait()
+    for step in range(1, owners):
+        arrived(got.at[piece(other(step)), :], trace_recv.at[other(step)])
+    solve_fluxes(plane, per, got, back, lane_ref, join, by_row, by_col, col_table, row_table)
+    for step in range(1, owners):
+        flux_copy(step).start()
+    own_flux = pltpu.make_async_copy(
+        back.at[piece(me), :], flux_ref.at[piece(me), :], flux_recv.at[me]
+    )
+    own_flux.start()
+
+    def sent(row, carry):
         for step in range(1, shares):
             line_copy(row, step).wait_send()
             out_copy(row, step).wait_send()
-            source = peer(step)
-            arrived(out_ref.at[:, source * own_rows + row, :], out_recv.at[row, source])
-        own_copy(row).wait()
         return carry
 
-    lax.fori_loop(0, own_rows, finish, 0)
+    lax.fori_loop(0, own_rows, sent, 0)
     for condition, copy in remote_copies:
         if condition is None:
             copy.wait_send()
         else:
             pl.when(condition)(copy.wait_send)
-
-
-def galerkin_product(field, log_fields, weights, node_index, mode_index):
+    save.wait()
+    own_flux.wait()
+    for step in range(1, owners):
+        trace_copy(step).wait_send()
+        flux_copy(step).wait_send()
+        arrived(flux_ref.at[piece(other(step)), :], flux_recv.at[other(step)])
+
+
+def finish_kernel(
+    spec_ref, flux_ref, now_ref, before_ref, mean_ref, lane_ref, column_ref, rows_ref, cols_ref,
+    fresh_ref, update_ref, inverse,
+):
+    rows = spec_ref.shape[1]
+    column = lambda k: jnp.broadcast_to(column_ref[:rows, k : k + 1], (rows, LANES))
+
+    @pl.when(pl.program_id(0) == 0)
+    def start():
+        inverse[...] = 1.0 / (storage_rate + mean_ref[0] * (column(3) + lane_ref[2:3, :]))
+
+    upright = jnp.transpose(flux_ref[...])
+    for pair in range(spec_ref.shape[0]):
+        parts = []
+        for half in range(2):
+            beside = lambda kind: jnp.broadcast_to(
+                upright[half * rows : (half + 1) * rows, 8 * pair + kind : 8 * pair + kind + 1],
+                (rows, LANES),
+            )
+            over = lambda kind: flux_ref[8 * pair + kind : 8 * pair + kind + 1, :]
+            part = spec_ref[pair, :, half * LANES : (half + 1) * LANES]
+            part = part + (beside(1) * lane_ref[1:2, :] - beside(0) * lane_ref[0:1, :])
+            part = part + (column(5) * over(4 + half) - column(4) * over(2 + half))
+            parts.append(part * inverse[...])
+        high, low = split_two(jnp.concatenate(parts, axis=1))
+        part = product(rows_ref[...], jnp.concatenate([high, low, high], axis=0))
+        high, low = split_two(jnp.concatenate([part[:, :LANES], part[:, LANES:]], axis=0))
+        part = product(jnp.concatenate([high, low], axis=1), cols_ref[...])
+        part = (part[:, :LANES] + part[:, LANES:]).reshape(2, rows, LANES)
+        mode = slice(2 * pair, 2 * pair + 2)
+        update_ref[mode] = part
+        before = before_ref[mode]
+        fresh_ref[mode] = before + relax_weight * (now_ref[mode] - before + step_length * part)
+
+
+def cosine_table(length):
+    freq, cells = np.arange(length)[:, None], np.arange(length)[None, :]
+    factor = np.where(freq == 0, math.sqrt(1.0 / length), math.sqrt(2.0 / length))
+    return factor * np.cos((freq * (2 * cells + 1) % (4 * length)) * (math.pi / (2 * length)))
+
+
+def pieces(table):
+    found, rest = [], table.astype(np.float32)
+    for _ in range(3):
+        found.append(rest.astype(BF16))
+        rest = rest - found[-1].astype(np.float32)
+    return found
+
+
+def constant_tables(count_x, rows, width):
+    eigen = lambda count: 2.0 - 2.0 * np.cos(np.arange(count) * (math.pi / count))
+    row_table, col_table = cosine_table(rows), cosine_table(width)
+    far_table = cosine_table(count_x * width)
+    join = np.einsum("kix,lx->kil", far_table.reshape(-1, count_x, width), col_table)
+    twice = lambda a: np.concatenate([a, a])
+    lanes = [
+        col_table[:, 0], col_table[:, -1], eigen(width),
+        twice(row_table[:, 0]), twice(row_table[:, -1]), twice(eigen(rows)),
+    ]
+    columns = [lanes[2], lanes[0], lanes[1], lanes[5], lanes[3], lanes[4]]
+    grow = lambda a: np.pad(np.stack(a), ((0, 8 - len(a)), (0, 0))).astype(np.float32)
+    high, middle, low = pieces(col_table.T)
+    front = pieces(col_table)
+    pair = np.block([[high, middle], [high, middle]])
+    rest = np.concatenate([high, low])
+    back = np.block([[front[0], front[1]], [front[0], np.zeros_like(high)]])
+    high, middle, low = pieces(row_table)
+    every = np.concatenate([high, high, middle, middle, high, low], axis=1)
+    high, low, _ = pieces(row_table.T)
+    rows_back = np.concatenate([high, high, low], axis=1)
+    return dict(
+        pair=pair, rest=rest, every=every, lanes=grow(lanes), columns=grow(columns).T.copy(),
+        far=grow([eigen(count_x * width)]), join=join.reshape(len(far_table), -1).astype(np.float32),
+        rows=rows_back, cols=back,
+    )
+
+
+def chebyshev_step(
+    field, field_before, source, log_fields, weights, mean_perm, node_index, mode_index
+):
     modes, rows, width = field.shape
     count_x, count_y, shares = (lax.axis_size(axis) for axis in ("gx", "gy", "sa"))
     padded = round_up(modes, 16)
     grow = lambda a, size, dim: jnp.pad(
         a, [(0, size - a.shape[d] if d == dim else 0) for d in range(a.ndim)]
     )
-    field = grow(field, padded, 0)
+    field, field_before, source = (grow(a, padded, 0) for a in (field, field_before, source))
+    mean = mean_perm.reshape(1)
+    tables = constant_tables(count_x, rows, width)
+    pairs, owners = padded // 2, count_x * count_y
+    per = -(-pairs // owners)
+    depth_solve = round_up(count_y * per, 8)
+    extra = 8 * (depth_solve - count_y * per)
     own_rows = rows // shares
     nodes = node_index.shape[0]
     all_nodes = round_up(nodes, NODE_BLOCK)
@@ -440,11 +790,16 @@
     dma = lambda *shape: pltpu.SemaphoreType.DMA(shape)
     place = pl.BlockSpec(memory_space=pl.ANY)
     whole = pl.BlockSpec(memory_space=pltpu.VMEM)
-    result = pl.pallas_call(
+    numbers = pl.BlockSpec(memory_space=pltpu.SMEM)
+    spectrum, fluxes = pl.pallas_call(
         functools.partial(node_kernel, (count_x, count_y, shares, group)),
-        in_specs=[place, whole, place, whole, whole, whole, whole],
-        out_specs=place,
-        out_shape=jax.ShapeDtypeStruct((padded, rows, width), jnp.float32),
+        in_specs=[place, whole, place, whole, whole, whole, whole]
+        + [place, numbers] + [whole] * 6 + [place],
+        out_specs=[place, place],
+        out_shape=[
+            jax.ShapeDtypeStruct((pairs, rows, 2 * width), jnp.float32),
+            jax.ShapeDtypeStruct((owners * per * 8, LANES), jnp.float32),
+        ],
         scratch_shapes=[
             vmem((slots, shares, padded, LANES)),
             vmem((2, levels, LANES)),
@@ -460,6 +815,20 @@
             vmem((all_nodes, LANES)),
             vmem((all_nodes, LANES)),
             vmem((all_nodes, LANES)),
+            vmem((rows * padded, LANES)),
+            vmem((pairs, rows, 2 * LANES)),
+            vmem((padded, rows, LANES)),
+            vmem((owners * per * 8, LANES)),
+            vmem((owners * per * 8 + extra, LANES)),
+            vmem((owners * per * 8 + extra, LANES)),
+            vmem((LANES, LANES)),
+            vmem(tables["join"].shape),
+            vmem((rows, 2 * LANES)),
+            vmem((LANES, 4 * LANES)),
+            vmem((2 * LANES, 2 * LANES)),
+            vmem((count_x - 1, round_up(count_x - 1, 8), LANES)),
+            vmem((2 * count_y - 3, depth_solve, count_x * width)),
+            dma(2), pltpu.SemaphoreType.DMA, dma(owners), dma(owners), dma(owners), dma(owners),
             dma(own_rows, shares), dma(slots, shares), dma(2 * shares), dma(shares, 4),
             dma(4, shares), dma(4), dma(4), dma(own_rows, shares), dma(own_rows, shares),
         ],
@@ -468,9 +837,30 @@
         ),
     )(
         field, log_fields, cols, log_cols, germs, degrees,
-        grow(weights[None, :], all_nodes, 1),
-    )
-    return result[:modes]
+        grow(weights[None, :], all_nodes, 1), source, mean,
+        *(tables[name] for name in ("pair", "rest", "every", "lanes", "columns", "far", "join")),
+    )
+    step = math.gcd(pairs, 8)
+    block = pl.BlockSpec((2 * step, rows, width), lambda n: (n, 0, 0))
+    still = lambda a: pl.BlockSpec(a.shape, lambda n: (0,) * a.ndim)
+    shape = jax.ShapeDtypeStruct(field.shape, jnp.float32)
+    fresh, update = pl.pallas_call(
+        finish_kernel,
+        grid=(pairs // step,),
+        in_specs=[
+            pl.BlockSpec((step, rows, 2 * width), lambda n: (n, 0, 0)),
+            pl.BlockSpec((8 * step, LANES), lambda n: (n, 0)),
+            block, block, numbers,
+        ] + [still(tables[name]) for name in ("lanes", "columns", "rows", "cols")],
+        out_specs=[block, block],
+        out_shape=[shape, shape],
+        scratch_shapes=[vmem((rows, LANES))],
+        compiler_params=pltpu.CompilerParams(dimension_semantics=("arbitrary",)),
+    )(
+        spectrum, fluxes, field, field_before, mean,
+        *(tables[name] for name in ("lanes", "columns", "rows", "cols")),
+    )
+    return (fresh[:modes], update[:modes])
 
 
 def node_germs(node_index):
@@ -480,98 +870,9 @@
     return jnp.sum(picked * points, axis=2)
 
 
-def on_device(
-    field_now, field_before, source, log_fields, weights, mean_perm, node_index, mode_index
-):
-    galerkin = galerkin_product(field_now, log_fields, weights, node_index, mode_index)
-    update = precondition(source - galerkin, mean_perm)
-    fresh = field_before + relax_weight * (field_now - field_before + step_length * update)
-    return (fresh, update)
-
-
-def cosine_table(length):
-    freq, cells = np.arange(length)[:, None], np.arange(length)[None, :]
-    factor = np.where(freq == 0, math.sqrt(1.0 / length), math.sqrt(2.0 / length))
-    return factor * np.cos((freq * (2 * cells + 1) % (4 * length)) * (math.pi / (2 * length)))
-
-
-def flux_table(count, mean_perm, inverse, ends):
-    same = jnp.sum(inverse * ends[0] * ends[0], axis=0)
-    cross = jnp.sum(inverse * ends[0] * ends[1], axis=0)
-    number = np.arange(1, count)
-    sines = np.sin((number[:, None] * number[None, :]) % (2 * count) * (math.pi / count))
-    pairs = (2.0 / count) * sines[:, :, None] * sines[:, None, :]
-    turns = np.cos(number * (math.pi / count))
-    shrink = 1.0 / (1.0 / mean_perm + 2.0 * same - 2.0 * cross * turns[:, None].astype(np.float32))
-    table = jnp.sum(pairs[:, :, :, None].astype(np.float32) * shrink[:, None, None, :], axis=0)
-    return jnp.pad(table, ((1, 1), (0, 0), (0, 0)))
-
-
-def precondition(residual, mean_perm):
-    gy, gx = (lax.axis_size(axis) for axis in ("gy", "gx"))
-    modes, rows, width = residual.shape
-    f32 = lambda a: jnp.asarray(a.astype(np.float32))
-    row_table, col_table, whole_table = (cosine_table(n) for n in (rows, width, gx * width))
-    rows_matrix, cols_matrix = f32(row_table), f32(col_table)
-    row_ends, col_ends = f32(row_table[:, [0, -1]].T), f32(col_table[:, [0, -1]].T)
-    join = f32(np.einsum("kix,lx->kil", whole_table.reshape(-1, gx, width), col_table))
-    eigen = lambda count: 2.0 - 2.0 * np.cos(np.arange(count) * (math.pi / count))
-    denominator = lambda cols: storage_rate + mean_perm * f32(eigen(rows)[:, None] + cols[None, :])
-    inverse = 1.0 / denominator(eigen(width))
-    col_flux = flux_table(gx, mean_perm, inverse.T, col_ends[:, :, None])
-    row_flux = flux_table(gy, mean_perm, 1.0 / denominator(eigen(gx * width)), row_ends[:, :, None])
-    mix = lambda spec, *args: jnp.einsum(spec, *args, precision=HIGHEST)
-
-    spectral = mix("jy,myx->mjx", rows_matrix, residual)
-    spectral = mix("mjx,kx->mjk", spectral, cols_matrix)
-    alone = spectral * inverse
-    at_cols = mix("mjk,ck->mcj", alone, col_ends)
-    at_rows = mix("mjk,cj->mck", alone, row_ends)
-    sides = jnp.concatenate([at_cols.reshape(modes, -1), at_rows.reshape(modes, -1)], axis=1)
-    part = -(-modes // (gx * gy))
-    sides = jnp.pad(sides, ((0, gx * gy * part - modes), (0, 0)))
-    swap = lambda a: lax.all_to_all(a, ("gx", "gy"), split_axis=0, concat_axis=0, tiled=True)
-    every = swap(sides).reshape(gx, gy, part, -1)
-
-    def col_fluxes(ends):
-        jump = ends[1:, :, :, 0] - ends[:-1, :, :, 1]
-        return jnp.sum(col_flux[:, :, None, None, :] * jump[None], axis=1)
-
-    at_cols = every[..., : 2 * rows].reshape(gx, gy, part, 2, rows)
-    at_rows = every[..., 2 * rows :].reshape(gx, gy, part, 2, width)
-    through_cols = col_fluxes(at_cols)
-    by_row = inverse * row_ends[:, :, None]
-    by_col = inverse * col_ends[:, None, :]
-    at_rows = (
-        at_rows
-        + mix("iymj,cjk->iymck", through_cols[1:], by_row) * col_ends[1]
-        - mix("iymj,cjk->iymck", through_cols[:-1], by_row) * col_ends[0]
-    )
-    jump = at_rows[:, 1:, :, 0] - at_rows[:, :-1, :, 1]
-    jump = mix("kil,iyml->ymk", join, jump)
-    through_rows = jnp.sum(row_flux[:, :, None, :] * jump[None], axis=1)
-    through_rows = mix("kil,ymk->iyml", join, through_rows)
-    back = mix("iymk,cjk->iymcj", through_rows, by_col)
-    through_cols = through_cols + col_fluxes(
-        back[:, 1:] * row_ends[1] - back[:, :-1] * row_ends[0]
-    )
-    through = jnp.concatenate(
-        [through_cols[:-1], through_cols[1:], through_rows[:, :-1], through_rows[:, 1:]], axis=-1
-    )
-    through = swap(through.reshape(gx * gy * part, -1))[:modes, None, :]
-    left, right = through[..., :rows], through[..., rows : 2 * rows]
-    top, bottom = through[..., 2 * rows : -width], through[..., -width:]
-    upright = lambda a: jnp.swapaxes(a, 1, 2)
-    spectral = spectral + (upright(right) * col_ends[1] - upright(left) * col_ends[0])
-    spectral = spectral + (bottom * row_ends[1][:, None] - top * row_ends[0][:, None])
-    spectral = spectral * inverse
-    columns = mix("mjk,kx->mjx", spectral, cols_matrix)
-    return mix("jy,mjx->myx", rows_matrix, columns)
-
-
 def solution(mesh):
     return jax.shard_map(
-        on_device,
+        chebyshev_step,
         mesh=mesh,
         in_specs=(
             P("sa", "gy", "gx"),

time: 146 us -> 141 us (0.966)
  Pallas kernels: 72.2 us -> 122 us
  matrix products: 27 us -> 0 us
  blocking collectives: 11.6 us -> 0 us
  waiting for transfers between devices: 8.37 us -> 0 us
  starting transfers between devices: 5.13 us -> 0 us
  other arithmetic: 3.22 us -> 1.55 us
    pallas_call x1 -> x2, Pallas kernels: 72.2 us -> 122 us  [the longest x1 113 us: chebyshev_step(): pl.pallas_call(functools.partial(node_kernel, (count_x, count_y, shares,...]
    dot_general x11 -> x0, matrix products: 27 us -> none  [precondition(): mix = lambda spec, *args: jnp.einsum(spec, *args, precision=HIGHEST)]
    all_to_all x1 -> x0, blocking collectives: 11.6 us -> none  [precondition(): lax.all_to_all(a, ('gx', 'gy'), split_axis=0, concat_axis=0, tiled=True)]
    all_to_all x1 -> x0, waiting for transfers between devices: 8.37 us -> none  [precondition(): lax.all_to_all(a, ('gx', 'gy'), split_axis=0, concat_axis=0, tiled=True)]
    all_to_all x1 -> x0, starting transfers between devices: 5.13 us -> none  [precondition(): lax.all_to_all(a, ('gx', 'gy'), split_axis=0, concat_axis=0, tiled=True)]
    unnamed x42 -> x5, local copies, waits for them, and re-layouts: 6.53 us -> 6.33 us
    slice x6 -> x2, local copies, waits for them, and re-layouts: 6.23 us -> 6.23 us  [the longest x1 5.16 us: chebyshev_step(): field[:, :, 0]]
  transfers between devices with their start and end apart: 1 -> 0, of which waited for: 1 -> 0; matrix products, arithmetic and copies ran while one was open for 0% -> 0% of each run, Pallas kernels for 0% -> 0%
where the time goes in v1:
time: 141 us; the launch traced here: 140 us
  Pallas kernels  122 us (87%)
  local copies, waits for them, and re-layouts  15.3 us (11%)
  other arithmetic  1.55 us (1%)
    pallas_call x1, Pallas kernels, chebyshev_step(): pl.pallas_call(functools.partial(node_kernel, (count_x, count_y, shares,...  113 us
    pallas_call x1, Pallas kernels, chebyshev_step(): pl.pallas_call(finish_kernel, grid=(pairs // step,), in_specs=[pl.BlockSp...  9.59 us
    unnamed x5, local copies, waits for them, and re-layouts  6.33 us
    slice x1, local copies, waits for them, and re-layouts, chebyshev_step(): field[:, :, 0]  5.16 us

profile of v1, /device:TPU:0, one launch (start us, length us, event | category | flops | bytes accessed | tf_op | source)
XLA Modules:
  0.0 140.3 jit_solution(9336188640689721582)
XLA Ops:
  1.3 0.7 broadcast_in_dim.2
  2.0 0.6 pad.19.weight_ref
  2.6 0.9 select_reduce_fusion
  3.5 0.6 pad.18.germ_ref
  4.1 1.4 %copy.44.degree_ref = s32[160,8]{1,0:T(8,128)} copy(s32[160,8]{0,1:T(8,128)} %param.25) | data formatting | bytes 10240 | tf_op args[7]
  5.6 1.1 fusion.1
  6.7 0.2 copy.47
  6.8 0.2 copy.48
  7.0 0.6 select_maximum_fusion.log_cols_ref
  7.6 5.2 %fusion = (f32[80,64,1]{2,1,0:T(8,128)}, f32[80,64,1]{2,1,0:T(8,128)S(1)}) fusion(f32[80,64,128]{2,1,0:T(8,128)} %now_ref.1), kind=kLoop, calls=%fused_computation.5 | loop fusion | bytes 81920 | tf_op jit(solution)/shard_map/slice | solution.py:781
  12.8 3.0 %copy.45 = f32[80,64,1]{0,1,2:T(8,128)S(1)} copy(f32[80,64,1]{2,1,0:T(8,128)} %get-tuple-element.6) | data formatting | bytes 40960
  15.8 1.5 %copy.46 = f32[80,64,1]{0,1,2:T(8,128)S(1)} copy(f32[80,64,1]{2,1,0:T(8,128)S(1)} %get-tuple-element.7) | data formatting | bytes 40960
  17.3 0.1 copy.41
  17.5 0.7 pad.16.field_cols_ref
  18.1 112.6 %shard_map.185 = (f32[40,64,256]{2,1,0:T(8,128)}, f32[384,128]{1,0:T(8,128)}) custom-call(f32[80,64,128]{2,1,0:T(8,128)} %now_ref.1, f32[9,32,128]{2,1,0:T(8,128)} %log_ref.1, f32[2,2,80,128]{3,2,1,0:T(8,128)} %pad.16.field_cols_ref, f32[2,9,128]{2,1,0:T(8,128)} %select_maximum_fusion.log_cols_ref, f32[8,1536]{1,0:T(8,128)} %pad.18.germ_ref, ...), custom_call_target="tpu_custom_call" | custom-call | tf_op jit(solution)/shard_map/pallas_call | solution.py:794
  130.7 9.6 %shard_map.186 = (f32[80,64,128]{2,1,0:T(8,128)}, f32[80,64,128]{2,1,0:T(8,128)}) custom-call(f32[40,64,256]{2,1,0:T(8,128)} %get-tuple-element.4.spec_ref, f32[384,128]{1,0:T(8,128)} %get-tuple-element.5.flux_ref, f32[80,64,128]{2,1,0:T(8,128)} %now_ref.1, f32[80,64,128]{2,1,0:T(8,128)} %before_ref.1, f32[1]{0:T(128)} %bitcast.8.mean_ref, ...), custom_call_target="tpu_custom_call" | custom-call | tf_op jit(solution)/shard_map/pallas_call | solution.py:847
  (1 shorter events, 0.0 us)

commit v2 on v1

--- a/solution.py
+++ b/solution.py
@@ -205,13 +205,14 @@
 
 
 def node_kernel(
-    sizes, field_ref, log_ref, field_cols_ref, log_cols_ref, germ_ref, degree_ref, weight_ref,
+    sizes, field_ref, log_ref, node_ref, mode_ref, weight_ref,
     source_ref, mean_ref, pair_ref, rest_ref, all_ref, lane_ref, column_ref, far_ref, join_ref,
     spec_ref, flux_ref,
     lines, log_lines, log_sides, sides, total, line_op, log_op, basis_op, germ_op, weight_op,
     edge, value_prev, half_prev, flux_prev,
     home, spectrum, origin, traces, got, back, tall, join,
     inverse, by_row, by_col, col_table, row_table,
+    block_field, field_cols, log_cols, picks, shares_of, degrees,
     load_sem, spec_sem, trace_send, trace_recv, flux_send, flux_recv,
     line_send, line_recv, halo_send, side_send, side_recv, log_send, log_recv, out_send, out_recv,
 ):
@@ -236,6 +237,13 @@
     def arrived(target, recv):
         pltpu.make_async_copy(target, target, recv).wait()
 
+    load_field = pltpu.make_async_copy(field_ref, block_field, load_sem.at[2])
+    load_field.start()
+    load_origin = pltpu.make_async_copy(source_ref, origin, load_sem.at[0])
+    load_origin.start()
+    load_join = pltpu.make_async_copy(join_ref, join, load_sem.at[1])
+    load_join.start()
+
     barrier = pltpu.get_barrier_semaphore()
     greet = lambda **place: pl.semaphore_signal(
         barrier, inc=1, device_id=place, device_id_type=pl.DeviceIdType.MESH
@@ -257,6 +265,38 @@
         def _():
             for step in range(1, shares):
                 greet(sa=peer(step), **place)
+    pairs = modes // 2
+    unroll = max(n for n in range(1, 6) if pairs % n == 0)
+    pick_row = lax.broadcasted_iota(jnp.int32, (16, 2 * LANES), 0)
+    pick_lane = lax.broadcasted_iota(jnp.int32, (16, 2 * LANES), 1) % LANES
+    first_pick = jnp.logical_and(pick_row == 0, pick_lane == 0)
+    last_pick = jnp.logical_and(pick_row == 1, pick_lane == LANES - 1)
+    pick = jnp.where(jnp.logical_or(first_pick, last_pick), 1.0, 0.0).astype(BF16)
+
+    def columns_of(block):
+        return lax.dot_general(
+            pick, jnp.concatenate(split_two(block), axis=1), (((1,), (1,)), ((), ())),
+            preferred_element_type=jnp.float32,
+        )
+
+    log_cols[...] = jnp.zeros_like(log_cols)
+    for level in range(log_ref.shape[0]):
+        found = columns_of(log_ref[level])
+        for end in range(2):
+            log_cols[end, level : level + 1, :own_rows] = found[end : end + 1, :]
+    load_field.wait()
+
+    def take_columns(index, carry):
+        for pair in range(unroll):
+            mode = 2 * (index * unroll + pair)
+            found = columns_of(block_field[pl.ds(mode, 2)].reshape(2 * rows, LANES))
+            for half in range(2):
+                part = pltpu.roll(found, LANES - rows, 1) if half else found
+                for end in range(2):
+                    field_cols[end, pl.ds(mode + half, 1), :] = part[end : end + 1, :]
+        return carry
+
+    lax.fori_loop(0, pairs // unroll, take_columns, 0)
     sides_met = sum(condition.astype(jnp.int32) for condition, _ in conditions)
     pl.semaphore_wait(barrier, owners - 1 + (shares - 1) * (1 + sides_met))
 
@@ -277,8 +317,8 @@
          dict(gy=flat_next[0], sa=flat_next[1])),
         (not_first, log_ref.at[:, 0, :], log_lines.at[0], 1,
          dict(gy=flat_last[0], sa=flat_last[1])),
-        (x < count_x - 1, log_cols_ref.at[1], log_sides.at[0], 2, dict(gx=x + 1)),
-        (x > 0, log_cols_ref.at[0], log_sides.at[1], 3, dict(gx=x - 1)),
+        (x < count_x - 1, log_cols.at[1], log_sides.at[0], 2, dict(gx=x + 1)),
+        (x > 0, log_cols.at[0], log_sides.at[1], 3, dict(gx=x - 1)),
     )
     for condition, source, target, slot, place in log_copies:
         start(condition, remote(source, target, log_send.at[slot], log_recv.at[slot], **place))
@@ -313,7 +353,7 @@
     for step in range(shares):
         to = peer(step)
         for kind in range(2):
-            source = field_cols_ref.at[to, kind]
+            source = field_cols.at[kind]
             if step:
                 start(None, remote(
                     source, sides.at[kind, share], side_send.at[step, kind],
@@ -324,11 +364,11 @@
                     source, sides.at[kind, share], side_recv.at[kind, share]
                 ).start()
         start(x > 0, remote(
-            field_cols_ref.at[to, 0], sides.at[2, share], side_send.at[step, 2],
+            field_cols.at[0], sides.at[2, share], side_send.at[step, 2],
             side_recv.at[2, share], gx=x - 1, sa=to,
         ))
         start(x < count_x - 1, remote(
-            field_cols_ref.at[to, 1], sides.at[3, share], side_send.at[step, 3],
+            field_cols.at[1], sides.at[3, share], side_send.at[step, 3],
             side_recv.at[3, share], gx=x + 1, sa=to,
         ))
 
@@ -348,11 +388,6 @@
         return carry
 
     lax.fori_loop(0, own_rows, send_lines, 0)
-    load_origin = pltpu.make_async_copy(source_ref, origin, load_sem.at[0])
-    load_origin.start()
-    load_join = pltpu.make_async_copy(join_ref, join, load_sem.at[1])
-    load_join.start()
-    pairs = modes // 2
     per = traces.shape[0] // 8 // owners
     plane = (count_x, count_y)
     beyond = got.shape[0] - traces.shape[0]
@@ -367,15 +402,32 @@
     weight_op[...] = jnp.zeros_like(weight_op)
     total[...] = jnp.zeros_like(total)
 
+    nodes_given = node_ref.shape[1]
+    picks[...] = jnp.zeros_like(picks)
+    picks[:, :nodes_given] = node_ref[...]
+    shares_of[...] = jnp.zeros_like(shares_of)
+    shares_of[:, :nodes_given] = weight_ref[...]
+    degrees[...] = jnp.zeros_like(degrees)
+    for start_at in range(0, every, LANES):
+        width_at = min(LANES, every - start_at)
+        degrees[start_at : start_at + mode_ref.shape[0], :width_at] = mode_ref[
+            :, start_at : start_at + width_at
+        ].astype(jnp.float32)
+        here = slice(start_at, start_at + LANES)
+        degrees[here, :] = jnp.transpose(degrees[here, :])
+
     def make_basis(block, carry):
         lanes = pl.ds(pl.multiple_of(block * LANES, LANES), LANES)
-        germs = germ_ref[:, lanes]
+        picked = picks[:, lanes]
+        germs = jnp.zeros(picked.shape, jnp.float32)
+        for level, point in enumerate(hermite_points):
+            germs = jnp.where(picked == level, point, germs)
         square = germs * germs
         second = (square - 1.0) / math.sqrt(2.0)
         third = (square * germs - 3.0 * germs) / math.sqrt(6.0)
         values = jnp.ones((every, LANES), jnp.float32)
         for germ in range(germs.shape[0]):
-            degree = jnp.broadcast_to(degree_ref[:, germ : germ + 1], (every, LANES))
+            degree = jnp.broadcast_to(degrees[:every, germ : germ + 1], (every, LANES))
             at = lambda table: jnp.broadcast_to(table[germ : germ + 1, :], (every, LANES))
             values = values * jnp.where(
                 degree == 0, 1.0,
@@ -385,7 +437,7 @@
         wide = lambda a: a.astype(jnp.float32)
         stack = stacked([wide(high), wide(high), wide(low)], basis_op.shape[1])
         basis_op[lanes, :] = jnp.transpose(stack).astype(BF16)
-        high, low = split_two(values * (2.0 * weight_ref[:, lanes]))
+        high, low = split_two(values * (2.0 * shares_of[:, lanes]))
         weight_op[:every, lanes] = high
         weight_op[every:, lanes] = low
         spread = stacked([-jnp.ones((1, LANES), jnp.float32), -germs], LOG_DEPTH)
@@ -444,8 +496,9 @@
             wait = lambda: arrived(sides.at[kind, source], side_recv.at[kind, source])
             wait() if condition is None else pl.when(condition)(wait)
     flat = lambda ref: ref.reshape(every, LANES)
-    side = [flat(sides[kind]) for kind in range(4)]
-    log_first, log_last = log_cols_ref[0], log_cols_ref[1]
+    turn = lax.rem(LANES - share * own_rows, LANES)
+    side = [pltpu.roll(flat(sides[kind]), turn, 1) for kind in range(4)]
+    log_first, log_last = log_cols[0], log_cols[1]
     before = jnp.where(x == 0, side[0], side[3])
     after = jnp.where(x == count_x - 1, side[1], side[2])
     log_before = jnp.where(x == 0, log_first, log_sides[0])
@@ -509,13 +562,17 @@
             total.at[row, share], home_row(share * own_rows + row), out_recv.at[row, share]
         )
 
-    def take_origin(pair, carry):
+    def take_origin(index, carry):
+        for pair in range(unroll):
+            one_origin(index * unroll + pair)
+        return carry
+
+    def one_origin(pair):
         block = origin[pl.ds(2 * pair, 2)].reshape(2 * rows, LANES)
         block = row_transform(block, pair_ref, rest_ref)
         spectrum[pair] = col_transform(
             jnp.concatenate([block[:rows], block[rows:]], axis=1), all_ref
         )
-        return carry
 
     groups = own_rows // group
     load_origin.wait()
@@ -523,7 +580,8 @@
     def take_group(index, carry):
         base = index * group
         lax.fori_loop(
-            lax.div(index * pairs, groups), lax.div((index + 1) * pairs, groups), take_origin, 0
+            lax.div(index * (pairs // unroll), groups),
+            lax.div((index + 1) * (pairs // unroll), groups), take_origin, 0,
         )
         for ahead in range(1, group + 1):
             row = base + ahead
@@ -623,7 +681,14 @@
         )
         return columns
 
-    columns = lax.fori_loop(0, pairs, take_pair, jnp.zeros((LANES, LANES), jnp.float32))
+    def take_pairs(index, columns):
+        for pair in range(unroll):
+            columns = take_pair(index * unroll + pair, columns)
+        return columns
+
+    columns = lax.fori_loop(
+        0, pairs // unroll, take_pairs, jnp.zeros((LANES, LANES), jnp.float32)
+    )
     tall[...] = jnp.transpose(columns)
     for end in range(2):
         traces[pl.ds(end, pairs, stride=8), :] = tall[pl.ds(end * (LANES // 2), pairs), :]
@@ -776,11 +841,7 @@
     own_rows = rows // shares
     nodes = node_index.shape[0]
     all_nodes = round_up(nodes, NODE_BLOCK)
-    germs = grow(node_germs(node_index).T, all_nodes, 1)
-    degrees = grow(mode_index.reshape(shares, modes, -1), padded, 1).reshape(shares * padded, -1)
-    cols = jnp.stack([field[:, :, 0], field[:, :, -1]]).reshape(2, padded, shares, own_rows)
-    cols = grow(cols.transpose(2, 0, 1, 3), LANES, 3)
-    log_cols = grow(jnp.stack([log_fields[:, :, 0], log_fields[:, :, -1]]), LANES, 2)
+    modes_of = grow(mode_index.reshape(shares, modes, -1), padded, 1).reshape(shares * padded, -1)
     levels = log_fields.shape[0]
     group = math.gcd(own_rows, 8)
     every = shares * padded
@@ -793,7 +854,7 @@
     numbers = pl.BlockSpec(memory_space=pltpu.SMEM)
     spectrum, fluxes = pl.pallas_call(
         functools.partial(node_kernel, (count_x, count_y, shares, group)),
-        in_specs=[place, whole, place, whole, whole, whole, whole]
+        in_specs=[place, whole, whole, whole, whole]
         + [place, numbers] + [whole] * 6 + [place],
         out_specs=[place, place],
         out_shape=[
@@ -828,7 +889,13 @@
             vmem((2 * LANES, 2 * LANES)),
             vmem((count_x - 1, round_up(count_x - 1, 8), LANES)),
             vmem((2 * count_y - 3, depth_solve, count_x * width)),
-            dma(2), pltpu.SemaphoreType.DMA, dma(owners), dma(owners), dma(owners), dma(owners),
+            vmem((padded, rows, LANES)),
+            vmem((2, padded, LANES)),
+            vmem((2, levels, LANES)),
+            vmem((node_index.shape[1], all_nodes), jnp.int32),
+            vmem((1, all_nodes)),
+            vmem((round_up(every, LANES), LANES)),
+            dma(3), pltpu.SemaphoreType.DMA, dma(owners), dma(owners), dma(owners), dma(owners),
             dma(own_rows, shares), dma(slots, shares), dma(2 * shares), dma(shares, 4),
             dma(4, shares), dma(4), dma(4), dma(own_rows, shares), dma(own_rows, shares),
         ],
@@ -836,8 +903,7 @@
             collective_id=0, has_side_effects=True, vmem_limit_bytes=56 * 1024 * 1024
         ),
     )(
-        field, log_fields, cols, log_cols, germs, degrees,
-        grow(weights[None, :], all_nodes, 1), source, mean,
+        field, log_fields, node_index.T, modes_of.T, weights[None, :], source, mean,
         *(tables[name] for name in ("pair", "rest", "every", "lanes", "columns", "far", "join")),
     )
     step = math.gcd(pairs, 8)
@@ -863,13 +929,6 @@
     return (fresh[:modes], update[:modes])
 
 
-def node_germs(node_index):
-    levels = jnp.arange(len(hermite_points), dtype=jnp.int32)
-    picked = (node_index[:, :, None] == levels).astype(jnp.float32)
-    points = jnp.asarray(hermite_points, dtype=jnp.float32)
-    return jnp.sum(picked * points, axis=2)
-
-
 def solution(mesh):
     return jax.shard_map(
         chebyshev_step,

time: 141 us -> 116 us (0.82)
  local copies, waits for them, and re-layouts: 15.3 us -> 1.29 us
  Pallas kernels: 122 us -> 113 us
  other arithmetic: 1.55 us -> 0 us
    pallas_call x1, Pallas kernels: 113 us -> 103 us  [chebyshev_step(): pl.pallas_call(functools.partial(node_kernel, (count_x, count_y, shares,...]
    unnamed x5 -> x0, local copies, waits for them, and re-layouts: 6.33 us -> none
    slice x2 -> x0, local copies, waits for them, and re-layouts: 6.23 us -> none  [the longest x1 5.16 us: chebyshev_step(): field[:, :, 0]]
    pad x3 -> x0, local copies, waits for them, and re-layouts: 1.91 us -> none  [chebyshev_step(): jnp.pad(a, [(0, size - a.shape[d] if d == dim else 0) for d in range(a.nd...]
where the time goes in v2:
time: 116 us; the launch traced here: 115 us
  Pallas kernels  113 us (97%)
  local copies, waits for them, and re-layouts  1.29 us (1%)
  between operations  1.29 us (1%)
    pallas_call x1, Pallas kernels, chebyshev_step(): pl.pallas_call(functools.partial(node_kernel, (count_x, count_y, shares,...  103 us
    pallas_call x1, Pallas kernels, chebyshev_step(): pl.pallas_call(finish_kernel, grid=(pairs // step,), in_specs=[pl.BlockSp...  9.59 us

profile of v2, /device:TPU:0, one launch (start us, length us, event | category | flops | bytes accessed | tf_op | source)
XLA Modules:
  0.0 115.5 jit_solution(11263878955821206235)
XLA Ops:
  1.3 1.3 %broadcast_in_dim.3.weight_ref = f32[1,1500]{1,0:T(1,128)} reshape(f32[1500]{0:T(1024)} %param.21) | data formatting | bytes 12000 | tf_op jit(solution)/shard_map/broadcast_in_dim | solution.py:906
  2.6 103.3 %shard_map.176 = (f32[40,64,256]{2,1,0:T(8,128)}, f32[384,128]{1,0:T(8,128)}) custom-call(f32[80,64,128]{2,1,0:T(8,128)} %now_ref.1, f32[9,32,128]{2,1,0:T(8,128)} %log_ref.1, s32[8,1500]{1,0:T(8,128)} %bitcast.5, s32[8,160]{1,0:T(8,128)} %bitcast.6, f32[1,1500]{1,0:T(1,128)} %broadcast_in_dim.3.weight_ref, f32[80,64,128]{2,1,0:T(8,128)} %source_ref.1, ...), custom_call_target="tpu_custom_call" | custom-call | tf_op jit(solution)/shard_map/pallas_call | solution.py:855
  105.9 9.6 %shard_map.177 = (f32[80,64,128]{2,1,0:T(8,128)}, f32[80,64,128]{2,1,0:T(8,128)}) custom-call(f32[40,64,256]{2,1,0:T(8,128)} %get-tuple-element.4.spec_ref, f32[384,128]{1,0:T(8,128)} %get-tuple-element.5.flux_ref, f32[80,64,128]{2,1,0:T(8,128)} %now_ref.1, f32[80,64,128]{2,1,0:T(8,128)} %before_ref.1, f32[1]{0:T(128)} %bitcast.4.mean_ref, ...), custom_call_target="tpu_custom_call" | custom-call | tf_op jit(solution)/shard_map/pallas_call | solution.py:913

commit v3 on v2

--- a/solution.py
+++ b/solution.py
@@ -28,6 +28,7 @@
 LANES = 128
 NODE_BLOCK = 512
 LOG_DEPTH = 16
+EARLY = 4
 BF16 = jnp.bfloat16
 
 
@@ -265,38 +266,6 @@
         def _():
             for step in range(1, shares):
                 greet(sa=peer(step), **place)
-    pairs = modes // 2
-    unroll = max(n for n in range(1, 6) if pairs % n == 0)
-    pick_row = lax.broadcasted_iota(jnp.int32, (16, 2 * LANES), 0)
-    pick_lane = lax.broadcasted_iota(jnp.int32, (16, 2 * LANES), 1) % LANES
-    first_pick = jnp.logical_and(pick_row == 0, pick_lane == 0)
-    last_pick = jnp.logical_and(pick_row == 1, pick_lane == LANES - 1)
-    pick = jnp.where(jnp.logical_or(first_pick, last_pick), 1.0, 0.0).astype(BF16)
-
-    def columns_of(block):
-        return lax.dot_general(
-            pick, jnp.concatenate(split_two(block), axis=1), (((1,), (1,)), ((), ())),
-            preferred_element_type=jnp.float32,
-        )
-
-    log_cols[...] = jnp.zeros_like(log_cols)
-    for level in range(log_ref.shape[0]):
-        found = columns_of(log_ref[level])
-        for end in range(2):
-            log_cols[end, level : level + 1, :own_rows] = found[end : end + 1, :]
-    load_field.wait()
-
-    def take_columns(index, carry):
-        for pair in range(unroll):
-            mode = 2 * (index * unroll + pair)
-            found = columns_of(block_field[pl.ds(mode, 2)].reshape(2 * rows, LANES))
-            for half in range(2):
-                part = pltpu.roll(found, LANES - rows, 1) if half else found
-                for end in range(2):
-                    field_cols[end, pl.ds(mode + half, 1), :] = part[end : end + 1, :]
-        return carry
-
-    lax.fori_loop(0, pairs // unroll, take_columns, 0)
     sides_met = sum(condition.astype(jnp.int32) for condition, _ in conditions)
     pl.semaphore_wait(barrier, owners - 1 + (shares - 1) * (1 + sides_met))
 
@@ -312,16 +281,6 @@
     row_of = lambda row: field_ref.at[:, row, :]
     flat_next = jnp.where(share == shares - 1, y + 1, y), lax.rem(share + 1, shares)
     flat_last = jnp.where(share == 0, y - 1, y), lax.rem(share + shares - 1, shares)
-    log_copies = (
-        (not_last, log_ref.at[:, own_rows - 1, :], log_lines.at[1], 0,
-         dict(gy=flat_next[0], sa=flat_next[1])),
-        (not_first, log_ref.at[:, 0, :], log_lines.at[0], 1,
-         dict(gy=flat_last[0], sa=flat_last[1])),
-        (x < count_x - 1, log_cols.at[1], log_sides.at[0], 2, dict(gx=x + 1)),
-        (x > 0, log_cols.at[0], log_sides.at[1], 3, dict(gx=x - 1)),
-    )
-    for condition, source, target, slot, place in log_copies:
-        start(condition, remote(source, target, log_send.at[slot], log_recv.at[slot], **place))
     start(y > 0, remote(
         row_of(0), lines.at[below, share], halo_send.at[0], line_recv.at[below, share],
         gy=y - 1, sa=jnp.int32(shares - 1),
@@ -350,6 +309,65 @@
     )
     pl.when(share > 0)(own_above.start)
     pl.when(share < shares - 1)(own_below.start)
+    def line_copy(row, step):
+        to = peer(step)
+        return remote(
+            row_of(to * own_rows + row), lines.at[row, share], line_send.at[row, step],
+            line_recv.at[row, share], sa=to,
+        )
+
+    def send_lines(row, carry):
+        for step in range(1, shares):
+            line_copy(row, step).start()
+        pltpu.make_async_copy(
+            row_of(share * own_rows + row), lines.at[row, share], line_recv.at[row, share]
+        ).start()
+        return carry
+
+    early = min(EARLY, own_rows)
+    lax.fori_loop(0, early, send_lines, 0)
+    pairs = modes // 2
+    unroll = max(n for n in range(1, 6) if pairs % n == 0)
+    pick_row = lax.broadcasted_iota(jnp.int32, (16, 2 * LANES), 0)
+    pick_lane = lax.broadcasted_iota(jnp.int32, (16, 2 * LANES), 1) % LANES
+    first_pick = jnp.logical_and(pick_row == 0, pick_lane == 0)
+    last_pick = jnp.logical_and(pick_row == 1, pick_lane == LANES - 1)
+    pick = jnp.where(jnp.logical_or(first_pick, last_pick), 1.0, 0.0).astype(BF16)
+
+    def columns_of(block):
+        return lax.dot_general(
+            pick, jnp.concatenate(split_two(block), axis=1), (((1,), (1,)), ((), ())),
+            preferred_element_type=jnp.float32,
+        )
+
+    log_cols[...] = jnp.zeros_like(log_cols)
+    for level in range(log_ref.shape[0]):
+        found = columns_of(log_ref[level])
+        for end in range(2):
+            log_cols[end, level : level + 1, :own_rows] = found[end : end + 1, :]
+    load_field.wait()
+
+    def take_columns(index, carry):
+        for pair in range(unroll):
+            mode = 2 * (index * unroll + pair)
+            found = columns_of(block_field[pl.ds(mode, 2)].reshape(2 * rows, LANES))
+            for half in range(2):
+                part = pltpu.roll(found, LANES - rows, 1) if half else found
+                for end in range(2):
+                    field_cols[end, pl.ds(mode + half, 1), :] = part[end : end + 1, :]
+        return carry
+
+    lax.fori_loop(0, pairs // unroll, take_columns, 0)
+    log_copies = (
+        (not_last, log_ref.at[:, own_rows - 1, :], log_lines.at[1], 0,
+         dict(gy=flat_next[0], sa=flat_next[1])),
+        (not_first, log_ref.at[:, 0, :], log_lines.at[0], 1,
+         dict(gy=flat_last[0], sa=flat_last[1])),
+        (x < count_x - 1, log_cols.at[1], log_sides.at[0], 2, dict(gx=x + 1)),
+        (x > 0, log_cols.at[0], log_sides.at[1], 3, dict(gx=x - 1)),
+    )
+    for condition, source, target, slot, place in log_copies:
+        start(condition, remote(source, target, log_send.at[slot], log_recv.at[slot], **place))
     for step in range(shares):
         to = peer(step)
         for kind in range(2):
@@ -372,22 +390,7 @@
             side_recv.at[3, share], gx=x + 1, sa=to,
         ))
 
-    def line_copy(row, step):
-        to = peer(step)
-        return remote(
-            row_of(to * own_rows + row), lines.at[row, share], line_send.at[row, step],
-            line_recv.at[row, share], sa=to,
-        )
-
-    def send_lines(row, carry):
-        for step in range(1, shares):
-            line_copy(row, step).start()
-        pltpu.make_async_copy(
-            row_of(share * own_rows + row), lines.at[row, share], line_recv.at[row, share]
-        ).start()
-        return carry
-
-    lax.fori_loop(0, own_rows, send_lines, 0)
+    lax.fori_loop(early, own_rows, send_lines, 0)
     per = traces.shape[0] // 8 // owners
     plane = (count_x, count_y)
     beyond = got.shape[0] - traces.shape[0]
@@ -575,14 +578,9 @@
         )
 
     groups = own_rows // group
-    load_origin.wait()
 
     def take_group(index, carry):
         base = index * group
-        lax.fori_loop(
-            lax.div(index * (pairs // unroll), groups),
-            lax.div((index + 1) * (pairs // unroll), groups), take_origin, 0,
-        )
         for ahead in range(1, group + 1):
             row = base + ahead
             if ahead < group:
@@ -632,7 +630,7 @@
             flux_prev[nodes, :] = flux_up
             return carry
 
-        lax.fori_loop(0, blocks, take_nodes, 0)
+        lax.fori_loop(0, blocks, take_nodes, 0, unroll=True)
         lane = lax.broadcasted_iota(jnp.int32, (every, LANES), 1)
         for step in range(group):
             row = base + step
@@ -648,7 +646,9 @@
             own_copy(row).start()
         return carry
 
-    lax.fori_loop(0, own_rows // group, take_group, 0)
+    lax.fori_loop(0, groups, take_group, 0)
+    load_origin.wait()
+    lax.fori_loop(0, pairs // unroll, take_origin, 0)
 
     def arrive(row, carry):
         for step in range(1, shares):

time: 116 us -> 104 us (0.90)
  Pallas kernels: 113 us -> 101 us
    pallas_call x1, Pallas kernels: 103 us -> 91.8 us  [chebyshev_step(): pl.pallas_call(functools.partial(node_kernel, (count_x, count_y, shares,...]
where the time goes in v3:
time: 104 us
  Pallas kernels  101 us (97%)
  local copies, waits for them, and re-layouts  1.29 us (1%)
  between operations  1.29 us (1%)
    pallas_call x1, Pallas kernels, chebyshev_step(): pl.pallas_call(functools.partial(node_kernel, (count_x, count_y, shares,...  91.8 us
    pallas_call x1, Pallas kernels, chebyshev_step(): pl.pallas_call(finish_kernel, grid=(pairs // step,), in_specs=[pl.BlockSp...  9.59 us

profile of v3, /device:TPU:0, one launch (start us, length us, event | category | flops | bytes accessed | tf_op | source)
XLA Modules:
  0.0 103.9 jit_solution(15047489699269666253)
XLA Ops:
  1.3 1.3 %broadcast_in_dim.3.weight_ref = f32[1,1500]{1,0:T(1,128)} reshape(f32[1500]{0:T(1024)} %param.21) | data formatting | bytes 12000 | tf_op jit(solution)/shard_map/broadcast_in_dim | solution.py:906
  2.6 91.8 %shard_map.176 = (f32[40,64,256]{2,1,0:T(8,128)}, f32[384,128]{1,0:T(8,128)}) custom-call(f32[80,64,128]{2,1,0:T(8,128)} %now_ref.1, f32[9,32,128]{2,1,0:T(8,128)} %log_ref.1, s32[8,1500]{1,0:T(8,128)} %bitcast.5, s32[8,160]{1,0:T(8,128)} %bitcast.6, f32[1,1500]{1,0:T(1,128)} %broadcast_in_dim.3.weight_ref, f32[80,64,128]{2,1,0:T(8,128)} %source_ref.1, ...), custom_call_target="tpu_custom_call" | custom-call | tf_op jit(solution)/shard_map/pallas_call | solution.py:855
  94.3 9.6 %shard_map.177 = (f32[80,64,128]{2,1,0:T(8,128)}, f32[80,64,128]{2,1,0:T(8,128)}) custom-call(f32[40,64,256]{2,1,0:T(8,128)} %get-tuple-element.4.spec_ref, f32[384,128]{1,0:T(8,128)} %get-tuple-element.5.flux_ref, f32[80,64,128]{2,1,0:T(8,128)} %now_ref.1, f32[80,64,128]{2,1,0:T(8,128)} %before_ref.1, f32[1]{0:T(128)} %bitcast.4.mean_ref, ...), custom_call_target="tpu_custom_call" | custom-call | tf_op jit(solution)/shard_map/pallas_call | solution.py:913

commit v4 on v3

--- a/solution.py
+++ b/solution.py
@@ -327,7 +327,7 @@
     early = min(EARLY, own_rows)
     lax.fori_loop(0, early, send_lines, 0)
     pairs = modes // 2
-    unroll = max(n for n in range(1, 6) if pairs % n == 0)
+    unroll = max(n for n in range(1, 11) if pairs % n == 0)
     pick_row = lax.broadcasted_iota(jnp.int32, (16, 2 * LANES), 0)
     pick_lane = lax.broadcasted_iota(jnp.int32, (16, 2 * LANES), 1) % LANES
     first_pick = jnp.logical_and(pick_row == 0, pick_lane == 0)
@@ -711,15 +711,18 @@
             flux_recv.at[me], **at_owner(to),
         )
 
+    used = lambda owner: owner * per < pairs
     for step in range(1, owners):
-        trace_copy(step).start()
+        pl.when(used(other(step)))(trace_copy(step).start)
     got[piece(me), :] = traces[piece(me), :]
     load_join.wait()
     for step in range(1, owners):
-        arrived(got.at[piece(other(step)), :], trace_recv.at[other(step)])
+        @pl.when(used(me))
+        def _():
+            arrived(got.at[piece(other(step)), :], trace_recv.at[other(step)])
     solve_fluxes(plane, per, got, back, lane_ref, join, by_row, by_col, col_table, row_table)
     for step in range(1, owners):
-        flux_copy(step).start()
+        pl.when(used(me))(flux_copy(step).start)
     own_flux = pltpu.make_async_copy(
         back.at[piece(me), :], flux_ref.at[piece(me), :], flux_recv.at[me]
     )
@@ -740,9 +743,12 @@
     save.wait()
     own_flux.wait()
     for step in range(1, owners):
-        trace_copy(step).wait_send()
-        flux_copy(step).wait_send()
-        arrived(flux_ref.at[piece(other(step)), :], flux_recv.at[other(step)])
+        pl.when(used(other(step)))(trace_copy(step).wait_send)
+        pl.when(used(me))(flux_copy(step).wait_send)
+
+        @pl.when(used(other(step)))
+        def _():
+            arrived(flux_ref.at[piece(other(step)), :], flux_recv.at[other(step)])
 
 
 def finish_kernel(
@@ -903,10 +909,10 @@
             collective_id=0, has_side_effects=True, vmem_limit_bytes=56 * 1024 * 1024
         ),
     )(
-        field, log_fields, node_index.T, modes_of.T, weights[None, :], source, mean,
+        field, log_fields, node_index.T, modes_of.T, weights.reshape(1, -1), source, mean,
         *(tables[name] for name in ("pair", "rest", "every", "lanes", "columns", "far", "join")),
     )
-    step = math.gcd(pairs, 8)
+    step = math.gcd(pairs, 20)
     block = pl.BlockSpec((2 * step, rows, width), lambda n: (n, 0, 0))
     still = lambda a: pl.BlockSpec(a.shape, lambda n: (0,) * a.ndim)
     shape = jax.ShapeDtypeStruct(field.shape, jnp.float32)

time: 104 us -> 100 us (0.962)
  Pallas kernels: 101 us -> 97.5 us
    pallas_call x1, Pallas kernels: 91.8 us -> 89.6 us  [chebyshev_step(): pl.pallas_call(functools.partial(node_kernel, (count_x, count_y, shares,...]
    pallas_call x1, Pallas kernels: 9.59 us -> 7.93 us  [chebyshev_step(): pl.pallas_call(finish_kernel, grid=(pairs // step,), in_specs=[pl.BlockSp...]
    broadcast_in_dim x1 -> x0, local copies, waits for them, and re-layouts: 1.29 us -> none  [chebyshev_step(): weights[None, :]]
    reshape x0 -> x1, local copies, waits for them, and re-layouts: none -> 1.29 us  [chebyshev_step(): weights.reshape(1, -1)]
where the time goes in v4:
time: 100 us
  Pallas kernels  97.5 us (98%)
  local copies, waits for them, and re-layouts  1.29 us (1%)
  between operations  1.29 us (1%)
    pallas_call x1, Pallas kernels, chebyshev_step(): pl.pallas_call(functools.partial(node_kernel, (count_x, count_y, shares,...  89.6 us
    pallas_call x1, Pallas kernels, chebyshev_step(): pl.pallas_call(finish_kernel, grid=(pairs // step,), in_specs=[pl.BlockSp...  7.93 us

profile of v4, /device:TPU:0, one launch (start us, length us, event | category | flops | bytes accessed | tf_op | source)
XLA Modules:
  0.0 100.1 jit_solution(10847350758484422467)
XLA Ops:
  1.3 1.3 %reshape.12.weight_ref = f32[1,1500]{1,0:T(1,128)} reshape(f32[1500]{0:T(1024)} %param.21) | data formatting | bytes 12000 | tf_op jit(solution)/shard_map/reshape | solution.py:912
  2.6 89.6 %shard_map.176 = (f32[40,64,256]{2,1,0:T(8,128)}, f32[384,128]{1,0:T(8,128)}) custom-call(f32[80,64,128]{2,1,0:T(8,128)} %now_ref.1, f32[9,32,128]{2,1,0:T(8,128)} %log_ref.1, s32[8,1500]{1,0:T(8,128)} %bitcast.5, s32[8,160]{1,0:T(8,128)} %bitcast.6, f32[1,1500]{1,0:T(1,128)} %reshape.12.weight_ref, f32[80,64,128]{2,1,0:T(8,128)} %source_ref.1, ...), custom_call_target="tpu_custom_call" | custom-call | tf_op jit(solution)/shard_map/pallas_call | solution.py:861
  92.2 7.9 %shard_map.177 = (f32[80,64,128]{2,1,0:T(8,128)}, f32[80,64,128]{2,1,0:T(8,128)}) custom-call(f32[40,64,256]{2,1,0:T(8,128)} %get-tuple-element.4.spec_ref, f32[384,128]{1,0:T(8,128)} %get-tuple-element.5.flux_ref, f32[80,64,128]{2,1,0:T(8,128)} %now_ref.1, f32[80,64,128]{2,1,0:T(8,128)} %before_ref.1, f32[1]{0:T(128)} %bitcast.4.mean_ref, ...), custom_call_target="tpu_custom_call" | custom-call | tf_op jit(solution)/shard_map/pallas_call | solution.py:919

commit v5 on v4

--- a/solution.py
+++ b/solution.py
@@ -266,6 +266,33 @@
         def _():
             for step in range(1, shares):
                 greet(sa=peer(step), **place)
+    per = traces.shape[0] // 8 // owners
+    plane = (count_x, count_y)
+    beyond = got.shape[0] - traces.shape[0]
+    if beyond:
+        got[traces.shape[0] :, :] = jnp.zeros((beyond, LANES), jnp.float32)
+    traces[...] = jnp.zeros_like(traces)
+    make_tables(
+        plane, per, mean_ref[0], lane_ref, column_ref, far_ref,
+        inverse, by_row, by_col, col_table, row_table,
+    )
+
+    total[...] = jnp.zeros_like(total)
+
+    nodes_given = node_ref.shape[1]
+    picks[...] = jnp.zeros_like(picks)
+    picks[:, :nodes_given] = node_ref[...]
+    shares_of[...] = jnp.zeros_like(shares_of)
+    shares_of[:, :nodes_given] = weight_ref[...].reshape(1, nodes_given)
+    degrees[...] = jnp.zeros_like(degrees)
+    for start_at in range(0, every, LANES):
+        width_at = min(LANES, every - start_at)
+        degrees[start_at : start_at + mode_ref.shape[0], :width_at] = mode_ref[
+            :, start_at : start_at + width_at
+        ].astype(jnp.float32)
+        here = slice(start_at, start_at + LANES)
+        degrees[here, :] = jnp.transpose(degrees[here, :])
+
     sides_met = sum(condition.astype(jnp.int32) for condition, _ in conditions)
     pl.semaphore_wait(barrier, owners - 1 + (shares - 1) * (1 + sides_met))
 
@@ -347,6 +374,8 @@
             log_cols[end, level : level + 1, :own_rows] = found[end : end + 1, :]
     load_field.wait()
 
+    left_lanes = lax.broadcasted_iota(jnp.int32, (1, LANES), 1) < rows
+
     def take_columns(index, carry):
         for pair in range(unroll):
             mode = 2 * (index * unroll + pair)
@@ -355,6 +384,8 @@
                 part = pltpu.roll(found, LANES - rows, 1) if half else found
                 for end in range(2):
                     field_cols[end, pl.ds(mode + half, 1), :] = part[end : end + 1, :]
+                both = jnp.where(left_lanes, part[0:1, :], pltpu.roll(part, rows, 1)[1:2, :])
+                field_cols[2, pl.ds(mode + half, 1), :] = both
         return carry
 
     lax.fori_loop(0, pairs // unroll, take_columns, 0)
@@ -370,17 +401,15 @@
         start(condition, remote(source, target, log_send.at[slot], log_recv.at[slot], **place))
     for step in range(shares):
         to = peer(step)
-        for kind in range(2):
-            source = field_cols.at[kind]
-            if step:
-                start(None, remote(
-                    source, sides.at[kind, share], side_send.at[step, kind],
-                    side_recv.at[kind, share], sa=to,
-                ))
-            else:
-                pltpu.make_async_copy(
-                    source, sides.at[kind, share], side_recv.at[kind, share]
-                ).start()
+        if step:
+            start(None, remote(
+                field_cols.at[2], sides.at[0, share], side_send.at[step, 0],
+                side_recv.at[0, share], sa=to,
+            ))
+        else:
+            pltpu.make_async_copy(
+                field_cols.at[2], sides.at[0, share], side_recv.at[0, share]
+            ).start()
         start(x > 0, remote(
             field_cols.at[0], sides.at[2, share], side_send.at[step, 2],
             side_recv.at[2, share], gx=x - 1, sa=to,
@@ -391,34 +420,6 @@
         ))
 
     lax.fori_loop(early, own_rows, send_lines, 0)
-    per = traces.shape[0] // 8 // owners
-    plane = (count_x, count_y)
-    beyond = got.shape[0] - traces.shape[0]
-    if beyond:
-        got[traces.shape[0] :, :] = jnp.zeros((beyond, LANES), jnp.float32)
-    traces[...] = jnp.zeros_like(traces)
-    make_tables(
-        plane, per, mean_ref[0], lane_ref, column_ref, far_ref,
-        inverse, by_row, by_col, col_table, row_table,
-    )
-
-    weight_op[...] = jnp.zeros_like(weight_op)
-    total[...] = jnp.zeros_like(total)
-
-    nodes_given = node_ref.shape[1]
-    picks[...] = jnp.zeros_like(picks)
-    picks[:, :nodes_given] = node_ref[...]
-    shares_of[...] = jnp.zeros_like(shares_of)
-    shares_of[:, :nodes_given] = weight_ref[...]
-    degrees[...] = jnp.zeros_like(degrees)
-    for start_at in range(0, every, LANES):
-        width_at = min(LANES, every - start_at)
-        degrees[start_at : start_at + mode_ref.shape[0], :width_at] = mode_ref[
-            :, start_at : start_at + width_at
-        ].astype(jnp.float32)
-        here = slice(start_at, start_at + LANES)
-        degrees[here, :] = jnp.transpose(degrees[here, :])
-
     def make_basis(block, carry):
         lanes = pl.ds(pl.multiple_of(block * LANES, LANES), LANES)
         picked = picks[:, lanes]
@@ -493,14 +494,14 @@
 
     node_slice = lambda block: pl.ds(pl.multiple_of(block * NODE_BLOCK, NODE_BLOCK), NODE_BLOCK)
 
-    for kind in range(4):
-        condition = (None, None, x < count_x - 1, x > 0)[kind]
+    for kind, condition in ((0, None), (2, x < count_x - 1), (3, x > 0)):
         for source in range(shares):
             wait = lambda: arrived(sides.at[kind, source], side_recv.at[kind, source])
             wait() if condition is None else pl.when(condition)(wait)
     flat = lambda ref: ref.reshape(every, LANES)
     turn = lax.rem(LANES - share * own_rows, LANES)
-    side = [pltpu.roll(flat(sides[kind]), turn, 1) for kind in range(4)]
+    side = [pltpu.roll(flat(sides[kind]), turn, 1) for kind in (0, 0, 2, 3)]
+    side[1] = pltpu.roll(side[1], LANES - rows, 1)
     log_first, log_last = log_cols[0], log_cols[1]
     before = jnp.where(x == 0, side[0], side[3])
     after = jnp.where(x == count_x - 1, side[1], side[2])
@@ -896,7 +897,7 @@
             vmem((count_x - 1, round_up(count_x - 1, 8), LANES)),
             vmem((2 * count_y - 3, depth_solve, count_x * width)),
             vmem((padded, rows, LANES)),
-            vmem((2, padded, LANES)),
+            vmem((3, padded, LANES)),
             vmem((2, levels, LANES)),
             vmem((node_index.shape[1], all_nodes), jnp.int32),
             vmem((1, all_nodes)),
@@ -909,7 +910,7 @@
             collective_id=0, has_side_effects=True, vmem_limit_bytes=56 * 1024 * 1024
         ),
     )(
-        field, log_fields, node_index.T, modes_of.T, weights.reshape(1, -1), source, mean,
+        field, log_fields, node_index.T, modes_of.T, weights, source, mean,
         *(tables[name] for name in ("pair", "rest", "every", "lanes", "columns", "far", "join")),
     )
     step = math.gcd(pairs, 20)

time: 100 us -> 98.1 us (0.981)
  local copies, waits for them, and re-layouts: 1.29 us -> 0 us
    reshape x1 -> x0, local copies, waits for them, and re-layouts: 1.29 us -> none  [chebyshev_step(): weights.reshape(1, -1)]
where the time goes in v5:
time: 98.1 us; the launch traced here: 97.9 us
  Pallas kernels  96.7 us (99%)
  between operations  1.29 us (1%)
    pallas_call x1, Pallas kernels, chebyshev_step(): pl.pallas_call(functools.partial(node_kernel, (count_x, count_y, shares,...  88.7 us
    pallas_call x1, Pallas kernels, chebyshev_step(): pl.pallas_call(finish_kernel, grid=(pairs // step,), in_specs=[pl.BlockSp...  7.93 us

profile of v5, /device:TPU:0, one launch (start us, length us, event | category | flops | bytes accessed | tf_op | source)
XLA Modules:
  0.0 97.9 jit_solution(5263721842063888028)
XLA Ops:
  1.3 88.7 %shard_map.176 = (f32[40,64,256]{2,1,0:T(8,128)}, f32[384,128]{1,0:T(8,128)}) custom-call(f32[80,64,128]{2,1,0:T(8,128)} %now_ref.1, f32[9,32,128]{2,1,0:T(8,128)} %log_ref.1, s32[8,1500]{1,0:T(8,128)} %bitcast.5, s32[8,160]{1,0:T(8,128)} %bitcast.6, f32[1500]{0:T(1024)} %weight_ref.1, f32[80,64,128]{2,1,0:T(8,128)} %source_ref.1, f32[1]{0:T(128)} %bitcast.3.mean_ref, ...), custom_call_target="tpu_custom_call" | custom-call | tf_op jit(solution)/shard_map/pallas_call | solution.py:862
  90.0 7.9 %shard_map.177 = (f32[80,64,128]{2,1,0:T(8,128)}, f32[80,64,128]{2,1,0:T(8,128)}) custom-call(f32[40,64,256]{2,1,0:T(8,128)} %get-tuple-element.4.spec_ref, f32[384,128]{1,0:T(8,128)} %get-tuple-element.5.flux_ref, f32[80,64,128]{2,1,0:T(8,128)} %now_ref.1, f32[80,64,128]{2,1,0:T(8,128)} %before_ref.1, f32[1]{0:T(128)} %bitcast.4.mean_ref, ...), custom_call_target="tpu_custom_call" | custom-call | tf_op jit(solution)/shard_map/pallas_call | solution.py:920

commit v6 on v5

--- a/solution.py
+++ b/solution.py
@@ -26,7 +26,7 @@
 
 
 LANES = 128
-NODE_BLOCK = 512
+NODE_BLOCK = 768
 LOG_DEPTH = 16
 EARLY = 4
 BF16 = jnp.bfloat16
@@ -272,10 +272,6 @@
     if beyond:
         got[traces.shape[0] :, :] = jnp.zeros((beyond, LANES), jnp.float32)
     traces[...] = jnp.zeros_like(traces)
-    make_tables(
-        plane, per, mean_ref[0], lane_ref, column_ref, far_ref,
-        inverse, by_row, by_col, col_table, row_table,
-    )
 
     total[...] = jnp.zeros_like(total)
 
@@ -354,7 +350,7 @@
     early = min(EARLY, own_rows)
     lax.fori_loop(0, early, send_lines, 0)
     pairs = modes // 2
-    unroll = max(n for n in range(1, 11) if pairs % n == 0)
+    unroll = max(n for n in range(1, 21) if pairs % n == 0)
     pick_row = lax.broadcasted_iota(jnp.int32, (16, 2 * LANES), 0)
     pick_lane = lax.broadcasted_iota(jnp.int32, (16, 2 * LANES), 1) % LANES
     first_pick = jnp.logical_and(pick_row == 0, pick_lane == 0)
@@ -648,6 +644,10 @@
         return carry
 
     lax.fori_loop(0, groups, take_group, 0)
+    make_tables(
+        plane, per, mean_ref[0], lane_ref, column_ref, far_ref,
+        inverse, by_row, by_col, col_table, row_table,
+    )
     load_origin.wait()
     lax.fori_loop(0, pairs // unroll, take_origin, 0)
 

time: 98.1 us -> 97.7 us (level)
  no operation moved by 1% of the time
where the time goes in v6:
time: 97.7 us; the launch traced here: 97.5 us
  Pallas kernels  96.3 us (99%)
  between operations  1.29 us (1%)
    pallas_call x1, Pallas kernels, chebyshev_step(): pl.pallas_call(functools.partial(node_kernel, (count_x, count_y, shares,...  88.3 us
    pallas_call x1, Pallas kernels, chebyshev_step(): pl.pallas_call(finish_kernel, grid=(pairs // step,), in_specs=[pl.BlockSp...  7.93 us

profile of v6, /device:TPU:0, one launch (start us, length us, event | category | flops | bytes accessed | tf_op | source)
XLA Modules:
  0.0 97.5 jit_solution(4165903439671468599)
XLA Ops:
  1.3 88.3 %shard_map.176 = (f32[40,64,256]{2,1,0:T(8,128)}, f32[384,128]{1,0:T(8,128)}) custom-call(f32[80,64,128]{2,1,0:T(8,128)} %now_ref.1, f32[9,32,128]{2,1,0:T(8,128)} %log_ref.1, s32[8,1500]{1,0:T(8,128)} %bitcast.5, s32[8,160]{1,0:T(8,128)} %bitcast.6, f32[1500]{0:T(1024)} %weight_ref.1, f32[80,64,128]{2,1,0:T(8,128)} %source_ref.1, f32[1]{0:T(128)} %bitcast.3.mean_ref, ...), custom_call_target="tpu_custom_call" | custom-call | tf_op jit(solution)/shard_map/pallas_call | solution.py:862
  89.6 7.9 %shard_map.177 = (f32[80,64,128]{2,1,0:T(8,128)}, f32[80,64,128]{2,1,0:T(8,128)}) custom-call(f32[40,64,256]{2,1,0:T(8,128)} %get-tuple-element.4.spec_ref, f32[384,128]{1,0:T(8,128)} %get-tuple-element.5.flux_ref, f32[80,64,128]{2,1,0:T(8,128)} %now_ref.1, f32[80,64,128]{2,1,0:T(8,128)} %before_ref.1, f32[1]{0:T(128)} %bitcast.4.mean_ref, ...), custom_call_target="tpu_custom_call" | custom-call | tf_op jit(solution)/shard_map/pallas_call | solution.py:920
